TPU v7x, 128 devices: a whole 4x4x4 slice. The times are simulated.
128 devices in a mesh: row: 8 (over z, core), col: 16 (over x, y).
Axes of the slice: x: 4, y: 4, z: 4, core: 2. Of those that a mesh axis runs over, the one named last changes fastest.
Arguments:
- normed: bfloat16 [8192, 7168], P(None, 'col'), may hold values from -44 to 44
- projection_weight: bfloat16 [7168, 3, 7168], P('col', None, 'row')
- adapter_down_weight: bfloat16 [7168, 16, 32], P(None, 'col'), may hold values from -0.0625 to 0.0625
- adapter_up_weight: bfloat16 [16, 2, 16, 7168], P(None, None, None, 'row'), may hold values from -0.47851562 to 0.47851562
- packed_prompt_length: int32 [64], replicated, may hold values from 64 to 512, as said below
- prompt_adapter_ids: int32 [64], replicated, may hold values from 0 to 63, as said below
- slot_adapter_ids: int32 [16], replicated, may hold values from 0 to 63, as said below
- prompt_page_slots: int32 [64, 4], replicated, may hold values from -1 to 159, as said below
Outputs:
- attended: bfloat16 [8192, 7168], P('col', 'row')
- kv_cache: bfloat16 [160, 128, 2, 7168], P('col', None, None, 'row')
Inputs may be any that keep to these rules, and one draw needn't show every extreme that they name: `packed_prompt_length`: the 64 lengths sum to 8192; one of them is exactly 512 and one exactly 64. `slot_adapter_ids`: distinct adapter ids. `prompt_adapter_ids`: every entry is one of slot_adapter_ids, and every loaded adapter is named by at least one prompt. `prompt_page_slots`: entry [i, j] is -1 where 128 * j >= packed_prompt_length[i]; otherwise it lies among slots 10 * c to 10 * c + 9, where c is the block of 512 packed tokens that holds the page's last token. No slot is named twice.
All inputs are finite; a program needn't handle non-finite values.
Results may differ from a plain program's by a relative error of at most 0.0072.
Values may be sent and summed in bfloat16 or wider, within the bound.
A program may use at most 256 MiB of HBM per device.

v0:
```python
import jax
import jax.numpy as jnp
from jax import lax
from jax.sharding import PartitionSpec as P

HEAD_DIM = 128
PAGE = 128
NEAR = 1
SLOTS_DEV = 10


adapter_scale = 2.0
masked_score = -1e30


def shifted(block, axis, distance):
    devices = range(lax.axis_size(axis))
    route = [(i - distance, i) for i in devices if i - distance in devices]
    return lax.ppermute(block, axis, route)


def start_table(packed_prompt_length):
    prompt_ends = jnp.cumsum(packed_prompt_length)
    return prompt_ends - packed_prompt_length


def slot_table(prompt_adapter_ids, slot_adapter_ids):
    active_slots = slot_adapter_ids.shape[0]
    matched = slot_adapter_ids[None, :] == prompt_adapter_ids[:, None]
    return jnp.sum(
        jnp.where(matched, jnp.arange(active_slots, dtype=jnp.int32)[None, :], 0), axis=1
    )


def token_prompts(positions, prompt_starts):
    inside = (positions[:, None] >= prompt_starts[None, :]).astype(jnp.int32)
    return jnp.sum(inside, axis=1) - 1


def token_slots(prompts, slot_of):
    prompt_count = slot_of.shape[0]
    onehot = prompts[:, None] == jnp.arange(prompt_count, dtype=jnp.int32)[None, :]
    return jnp.sum(jnp.where(onehot, slot_of[None, :], 0), axis=1)


def down_term(row_block, slots_here, down_cols, active_slots):
    combined_output = jnp.dot(row_block, down_cols, preferred_element_type=jnp.float32)
    combined_output = combined_output.reshape(row_block.shape[0], active_slots, -1)
    pick_slot = slots_here[:, None] == jnp.arange(active_slots, dtype=jnp.int32)[None, :]
    return jnp.sum(jnp.where(pick_slot[:, :, None], combined_output, 0.0), axis=1)


def local(
    normed,
    projection_weight,
    adapter_down_weight,
    adapter_up_weight,
    packed_prompt_length,
    prompt_adapter_ids,
    slot_adapter_ids,
    prompt_page_slots,
):
    col_count = lax.axis_size("col")
    row_count = lax.axis_size("row")
    col_index = lax.axis_index("col")
    my_row = lax.axis_index("row")
    tok_all, width_loc = normed.shape
    tok_blk = tok_all // col_count
    head_column_span = projection_weight.shape[2]
    heads_loc = head_column_span // HEAD_DIM
    active_slots = slot_adapter_ids.shape[0]
    adapter_rank_width = adapter_up_weight.shape[2]
    prompt_starts = start_table(packed_prompt_length)
    slot_of = slot_table(prompt_adapter_ids, slot_adapter_ids)
    block_start = col_index * tok_blk
    mine = block_start + jnp.arange(tok_blk, dtype=jnp.int32)
    mine_prompts = token_prompts(mine, prompt_starts)
    mine_slots = token_slots(mine_prompts, slot_of)
    down_weight_slices = lax.all_to_all(
        adapter_down_weight, "col", split_axis=0, concat_axis=1, tiled=True
    )
    down_cols = down_weight_slices.reshape(width_loc, -1)
    own_rows = lax.all_to_all(normed, "col", split_axis=0, concat_axis=1, tiled=True)
    weight_piece = lax.all_gather(projection_weight, "col", axis=0, tiled=True)
    flat_piece = weight_piece.reshape(weight_piece.shape[0], -1)
    projection_total = jnp.dot(own_rows, flat_piece, preferred_element_type=jnp.float32)
    rows_per = tok_all // row_count
    row_first = my_row * rows_per
    row_positions = row_first + jnp.arange(rows_per, dtype=jnp.int32)
    row_slots = token_slots(token_prompts(row_positions, prompt_starts), slot_of)
    row_part = lax.dynamic_slice_in_dim(normed, row_first, rows_per, 0)
    summed = lax.psum(down_term(row_part, row_slots, down_cols, active_slots), "col")
    down_every = lax.all_gather(summed.astype(jnp.bfloat16), "row", axis=0, tiled=True)
    local_down_output = lax.dynamic_slice_in_dim(down_every, block_start, tok_blk, 0)
    pick_half = (mine_slots[:, None] == jnp.arange(active_slots, dtype=jnp.int32)[None, :]).astype(
        jnp.bfloat16
    )

    def reduced_rank_rows(low_part, slot_membership):
        token_spread = (pick_half[:, :, None] * low_part[:, None, :]).reshape(
            tok_blk, active_slots * adapter_rank_width
        )
        up_weight_table = adapter_up_weight[:, slot_membership].reshape(
            active_slots * adapter_rank_width, head_column_span
        )
        return jnp.dot(token_spread, up_weight_table, preferred_element_type=jnp.float32)

    query_token_rows = (
        projection_total[:, :head_column_span]
        + adapter_scale * reduced_rank_rows(local_down_output[:, :adapter_rank_width], 0)
    ).astype(jnp.bfloat16)
    key_rows = projection_total[:, head_column_span : 2 * head_column_span].astype(jnp.bfloat16)
    value_token_rows = (
        projection_total[:, 2 * head_column_span :]
        + adapter_scale * reduced_rank_rows(local_down_output[:, adapter_rank_width:], 1)
    ).astype(jnp.bfloat16)
    own_kv = jnp.stack([key_rows, value_token_rows], axis=1)
    earlier = [shifted(own_kv, "col", 1)]
    window = jnp.concatenate(earlier[::-1] + [own_kv], axis=0)
    window_len = window.shape[0]
    window_pos = block_start - NEAR * tok_blk + jnp.arange(window_len, dtype=jnp.int32)
    window_prompts = token_prompts(window_pos, prompt_starts)
    allowed = (mine_prompts[:, None] == window_prompts[None, :]) & (
        window_pos[None, :] <= mine[:, None]
    )
    query_heads = query_token_rows.reshape(tok_blk, heads_loc, HEAD_DIM)
    key_heads = window[:, 0].reshape(window_len, heads_loc, HEAD_DIM)
    value_heads = window[:, 1].reshape(window_len, heads_loc, HEAD_DIM)
    score_scale = HEAD_DIM ** (-0.5)
    scores = (
        jnp.einsum("qhd,khd->hqk", query_heads, key_heads, preferred_element_type=jnp.float32)
        * score_scale
    )
    limited = jnp.where(allowed[None], scores, masked_score)
    peak_score = jnp.max(limited, axis=2, keepdims=True)
    weight = jnp.where(allowed[None], jnp.exp(scores - peak_score), 0.0)
    denominator = jnp.sum(weight, axis=2)
    mixed_heads = jnp.einsum(
        "hqk,khd->qhd", weight.astype(jnp.bfloat16), value_heads, preferred_element_type=jnp.float32
    )
    attended = (
        (mixed_heads / jnp.transpose(denominator)[:, :, None])
        .reshape(tok_blk, head_column_span)
        .astype(jnp.bfloat16)
    )
    prev_kv = earlier[0]
    page_window = jnp.concatenate(
        [prev_kv, own_kv, jnp.zeros((PAGE, 2, head_column_span), jnp.bfloat16)], axis=0
    )
    max_pages = prompt_page_slots.shape[1]
    lens_rep = jnp.repeat(packed_prompt_length, max_pages)
    starts_rep = jnp.repeat(prompt_starts, max_pages)
    page_index = jnp.tile(jnp.arange(max_pages, dtype=jnp.int32), packed_prompt_length.shape[0])
    page_rows = jnp.clip(lens_rep - PAGE * page_index, 0, PAGE)
    page_first = starts_rep + PAGE * page_index
    my_slots = col_index * SLOTS_DEV + jnp.arange(SLOTS_DEV, dtype=jnp.int32)
    slot_hit = prompt_page_slots.reshape(-1)[None, :] == my_slots[:, None]
    rows_used = jnp.sum(jnp.where(slot_hit, page_rows[None, :], 0), axis=1)
    first_used = jnp.sum(jnp.where(slot_hit, page_first[None, :], 0), axis=1)
    offset = jnp.clip(first_used - (col_index - 1) * tok_blk, 0, 2 * tok_blk)
    page_lines = jnp.arange(PAGE, dtype=jnp.int32)
    pick_rows = (offset[:, None] + page_lines[None, :]).reshape(-1)
    taken_rows = jnp.take(page_window, pick_rows, axis=0).reshape(
        SLOTS_DEV, PAGE, 2, head_column_span
    )
    live_rows = (page_lines[None, :] < rows_used[:, None])[:, :, None, None]
    kv_pages = jnp.where(live_rows, taken_rows, jnp.zeros_like(taken_rows))
    return (attended, kv_pages)


def solution(mesh):
    placed = (
        P(None, "col"),
        P("col", None, "row"),
        P(None, "col", None),
        P(None, None, None, "row"),
        P(),
        P(),
        P(),
        P(),
    )
    return jax.shard_map(
        local,
        mesh=mesh,
        in_specs=placed,
        out_specs=(P("col", "row"), P("col", None, None, "row")),
        check_vma=False,
    )
```

profile of v0, /device:TPU:3, one launch (start us, length us, event | category | flops | bytes accessed | tf_op | source)
XLA Modules:
  0.0 537.2 jit_solution(5829252045479823222)
XLA Ops:
  7.2 0.7 all-gather.2.cloned.1.call-update
  7.9 0.5 broadcast.227
  8.4 1.9 reduce.3
  10.3 0.9 copy.105
  11.3 2.4 reshape.319
  13.7 6.9 %all-to-all-start.1 = ((bf16[16,2,7168]{2,1,0:T(2,128)(2,1)}), bf16[16,2,7168]{2,1,0:T(2,128)(2,1)S(1)}, u32[]{:S(2)}, u32[]{:S(2)}) async-start(bf16[16,2,7168]{2,1,0:T(2,128)(2,1)} %reshape.319), calls=%async_computation.1 | async-start | bytes 917504 | tf_op jit(solution)/shard_map/all_to_all | solution.py:79
  20.6 8.2 %copy.104 = bf16[56,16,8,512]{3,2,0,1:T(8,128)(2,1)} copy(bf16[56,16,8,512]{3,2,1,0:T(8,128)(2,1)} %bitcast.61) | data formatting | bytes 14680064 | tf_op jit(solution)/shard_map/all_to_all | solution.py:83
  28.8 6.8 %all-to-all-start = ((bf16[16,512,448]{1,2,0:T(8,128)(2,1)}), bf16[16,512,448]{1,2,0:T(8,128)(2,1)}, u32[]{:S(2)}, u32[]{:S(2)}) async-start(bf16[16,512,448]{1,2,0:T(8,128)(2,1)} %bitcast.59), calls=%async_computation | async-start | bytes 14680064 | tf_op jit(solution)/shard_map/all_to_all | solution.py:83
  35.6 0.1 copy.82
  35.7 0.1 reduce-window.9
  35.8 0.1 reduce
  36.1 0.1 convert_reduce_fusion.2
  36.2 0.1 select_reduce_fusion.3
  36.3 0.1 convert_reduce_fusion
  36.5 0.1 select_reduce_fusion.2
  36.8 4.2 reshape.320
  41.1 7.0 %copy.84 = bf16[7168,1,32]{0,2,1:T(8,128)(2,1)S(1)} copy(bf16[7168,1,32]{2,1,0:T(2,128)(2,1)} %reshape.320) | data formatting | bytes 917504 | tf_op jit(solution)/shard_map/all_to_all | solution.py:79
  48.1 0.6 all_to_all.30
  48.7 2.0 select_reduce_fusion.1
  50.7 186.5 %all-reduce.1 = bf16[1024,32]{0,1:T(8,128)(2,1)S(1)} all-reduce(f32[1024,32]{0,1:T(8,128)S(1)} %select_reduce_fusion.1), channel_id=1, replica_groups=mesh['row'=8,'col'=16] {'col'}, use_global_device_ids=true, to_apply=%region_7.8 | all-reduce | flops 32768 | bytes 196608 | tf_op jit(solution)/shard_map/psum | solution.py:92
  237.2 26.8 %all_gather.7 = bf16[8192,32]{0,1:T(8,128)(2,1)S(1)} all-gather(bf16[1024,32]{0,1:T(8,128)(2,1)S(1)} %all-reduce.1), channel_id=1, replica_groups=mesh['row'=8,'col'=16] {'row'}, dimensions={0}, use_global_device_ids=true | all-gather | bytes 589824 | tf_op jit(solution)/shard_map/all_gather | solution.py:93
  264.1 62.7 %all-gather.2.cloned.1.call-done = bf16[7168,3,896]{2,0,1:T(8,128)(2,1)} async-done(((bf16[448,3,896]{2,0,1:T(8,128)(2,1)}), bf16[7168,3,896]{2,0,1:T(8,128)(2,1)}) %all-gather.2.cloned.1.call-update) | async-done | bytes 38535184 | tf_op jit(solution)/shard_map/all_gather | solution.py:84
  326.9 51.4 %copy.81 = bf16[7168,3,896]{0,2,1:T(8,128)(2,1)} copy(bf16[7168,3,896]{2,0,1:T(8,128)(2,1)} %all-gather.2.cloned.1.call-done) | data formatting | bytes 77070336 | tf_op jit(solution)/shard_map/all_gather | solution.py:84
  378.2 28.4 %fusion.38 = f32[512,2688]{1,0:T(8,128)} fusion(bf16[512,7168]{0,1:T(8,128)(2,1)} %bitcast.1, bf16[7168,2688]{0,1:T(8,128)(2,1)} %bitcast.58), kind=kOutput, calls=%fused_computation.78 | convolution fusion | flops 19730006016 | bytes 51380224 | tf_op jit(solution)/shard_map/dot_general | solution.py:86
  406.6 1.6 fusion.16
  408.2 2.0 fusion.15
  410.2 1.4 pad_maximum_fusion
  411.6 1.9 collective-permute-start
  413.6 0.1 copy.91
  413.7 0.1 eq.123
  413.8 0.1 add.145
  413.9 0.1 min.20
  414.0 0.2 fusion.24
  414.5 1.3 compare_and_fusion
  415.8 2.0 fusion.10
  417.8 1.5 copy.87
  419.3 37.8 %collective-permute-done = bf16[512,2,896]{2,0,1:T(8,128)(2,1)} collective-permute-done((bf16[512,2,896]{2,0,1:T(8,128)(2,1)}, bf16[512,2,896]{2,0,1:T(8,128)(2,1)}, u32[]{:S(2)}, u32[]{:S(2)}) %collective-permute-start) | collective-permute-done | bytes 1835040 | tf_op jit(solution)/shard_map/ppermute | solution.py:19
  457.1 1.8 maximum_maximum_fusion.1
  458.8 2.1 fusion.35
  461.0 3.8 copy.88
  464.8 3.1 maximum_maximum_fusion
  468.0 15.3 %copy.92 = bf16[1152,2,896]{2,1,0:T(2,128)(2,1)} copy(bf16[1152,2,896]{2,0,1:T(8,128)(2,1)S(1)} %maximum_maximum_fusion) | data formatting | bytes 8257536 | tf_op jit(solution)/shard_map/concatenate | solution.py:147
  483.3 2.4 copy.86
  485.7 12.7 %fusion.37 = (f32[7,512]{1,0:T(8,128)S(1)}, bf16[7,512,1024]{2,1,0:T(8,128)(2,1)}) fusion(pred[512,1024]{1,0:T(8,128)(4,1)S(1)} %copy-done.4, bf16[512,7,128]{0,2,1:T(8,128)(2,1)S(1)} %bitcast.68, bf16[1024,7,128]{0,2,1:T(8,128)(2,1)} %bitcast.62), kind=kOutput, calls=%fused_computation.77 | convolution fusion | flops 1904739328 | bytes 10631168 | tf_op jit(solution)/shard_map/sub | solution.py:136
  498.4 5.7 %fusion.12 = bf16[512,7,128]{0,2,1:T(8,128)(2,1)S(1)} fusion(bf16[1024,7,128]{0,2,1:T(8,128)(2,1)S(1)} %bitcast.63, bf16[7,512,1024]{2,1,0:T(8,128)(2,1)} %get-tuple-element.29, f32[512,7]{0,1:T(8,128)S(1)} %bitcast.72), kind=kOutput, calls=%fused_computation.25 | convolution fusion | flops 940441600 | bytes 10106880 | tf_op jit(solution)/shard_map/hqk,khd->qhd/dot_general | solution.py:138
  504.0 1.3 copy.93
  505.3 16.6 %gather_fusion = bf16[1280,2,896]{2,1,0:T(2,128)(2,1)} fusion(bf16[1152,2,896]{2,1,0:T(2,128)(2,1)} %copy.92, s32[2048]{0:T(1024)S(1)} %pad_clamp_fusion), kind=kCustom, calls=%fused_computation | custom fusion | bytes 9180160 | tf_op jit(solution)/shard_map/jit(_take)/gather | solution.py:163
  521.9 8.5 %broadcast_select_fusion.1 = bf16[10,128,2,896]{3,2,1,0:T(2,128)(2,1)} fusion(pred[10,128]{1,0:T(8,128)(4,1)S(1)} %iota_compare_fusion.4, bf16[10,128,2,896]{3,2,1,0:T(2,128)(2,1)} %bitcast.60, pred[10,128]{1,0:T(8,128)(4,1)S(1)} %fusion.28), kind=kLoop, calls=%fused_computation.7 | loop fusion | flops 4587520 | bytes 9177600 | tf_op jit(solution)/shard_map/jit(_where)/select_n | solution.py:167
  (44 shorter events, 0.8 us)
Async XLA Ops:
  7.2 319.7 %all-gather.2.cloned.1.call-start = ((), (), s32[]{:S(2)}) async-start(), calls=%async_computation.2 | async-start | bytes 40943616 | tf_op jit(solution)/shard_map/all_gather | solution.py:84
  13.7 15.1 %all-to-all-start.1 = ((bf16[16,2,7168]{2,1,0:T(2,128)(2,1)}), bf16[16,2,7168]{2,1,0:T(2,128)(2,1)S(1)}, u32[]{:S(2)}, u32[]{:S(2)}) async-start(bf16[16,2,7168]{2,1,0:T(2,128)(2,1)} %reshape.319), calls=%async_computation.1 | async-start | bytes 917504 | tf_op jit(solution)/shard_map/all_to_all | solution.py:79
  28.8 6.8 %copy-start.5 = (s32[64]{0:T(128)S(1)}, s32[64]{0:T(128)}, u32[]{:S(2)}) copy-start(s32[64]{0:T(128)} %param.12) | copy-start | bytes 772
  28.8 7.2 %copy-start.7 = (s32[64]{0:T(128)S(1)}, s32[64]{0:T(128)}, u32[]{:S(2)}) copy-start(s32[64]{0:T(128)} %param.13) | copy-start | bytes 772
  28.8 7.2 %copy-start.8 = (s32[16]{0:T(128)S(1)}, s32[16]{0:T(128)}, u32[]{:S(2)}) copy-start(s32[16]{0:T(128)} %param.14) | copy-start | bytes 196
  28.8 7.9 %copy-start.2 = (bf16[16,2,16,896]{3,2,1,0:T(8,128)(2,1)S(1)}, bf16[16,2,16,896]{3,2,1,0:T(8,128)(2,1)}, u32[]{:S(2)}) copy-start(bf16[16,2,16,896]{3,2,1,0:T(8,128)(2,1)} %param.11) | copy-start | bytes 2752516
  28.8 349.4 %all-to-all-start = ((bf16[16,512,448]{1,2,0:T(8,128)(2,1)}), bf16[16,512,448]{1,2,0:T(8,128)(2,1)}, u32[]{:S(2)}, u32[]{:S(2)}) async-start(bf16[16,512,448]{1,2,0:T(8,128)(2,1)} %bitcast.59), calls=%async_computation | async-start | bytes 14680064 | tf_op jit(solution)/shard_map/all_to_all | solution.py:83
  406.6 7.0 %copy-start.6 = (s32[64,4]{0,1:T(4,128)S(1)}, s32[64,4]{0,1:T(4,128)}, u32[]{:S(2)}) copy-start(s32[64,4]{0,1:T(4,128)} %param.15) | copy-start | bytes 3076
  411.6 45.4 %collective-permute-start = (bf16[512,2,896]{2,0,1:T(8,128)(2,1)}, bf16[512,2,896]{2,0,1:T(8,128)(2,1)}, u32[]{:S(2)}, u32[]{:S(2)}) collective-permute-start(bf16[512,2,896]{2,0,1:T(8,128)(2,1)} %pad_maximum_fusion), channel_id=1, source_target_pairs={{0,1},{1,2},{2,3},{3,4},{4,5},{5,6},{6,7},{7,8},{8,9},{9,10},{10,1... | collective-permute-start | bytes 5505032 | tf_op jit(solution)/shard_map/ppermute | solution.py:19
  468.0 15.3 %copy-start = (bf16[1024,1,896]{2,0,1:T(8,128)(2,1)S(1)}, bf16[1024,1,896]{2,0,1:T(8,128)(2,1)}, u32[]{:S(2)}) copy-start(bf16[1024,1,896]{2,0,1:T(8,128)(2,1)} %get-tuple-element.21) | copy-start | bytes 5505028
  468.0 17.7 %copy-start.3 = (bf16[512,896]{0,1:T(8,128)(2,1)S(1)}, bf16[512,896]{0,1:T(8,128)(2,1)}, u32[]{:S(2)}) copy-start(bf16[512,896]{0,1:T(8,128)(2,1)} %copy.87) | copy-start | bytes 2752516
  468.0 17.7 %copy-start.4 = (pred[512,1024]{1,0:T(8,128)(4,1)S(1)}, pred[512,1024]{1,0:T(8,128)(4,1)}, u32[]{:S(2)}) copy-start(pred[512,1024]{1,0:T(8,128)(4,1)} %compare_and_fusion) | copy-start | bytes 1572868
  485.7 12.7 %copy-start.1 = (bf16[1024,1,896]{0,2,1:T(8,128)(2,1)S(1)}, bf16[1024,1,896]{0,2,1:T(8,128)(2,1)}, u32[]{:S(2)}) copy-start(bf16[1024,1,896]{0,2,1:T(8,128)(2,1)} %copy.86) | copy-start | bytes 5505028
Sparse Core Ops, SparseCore 0:
  10.1 316.6 all-gather.1
where the time goes:
time: 547 us; the launch traced here: 537 us
  blocking collectives  213 us (39%)
  local copies, waits for them, and re-layouts  121 us (22%)
  waiting for transfers between devices  101 us (18%)
  matrix products  52.6 us (10%)
  other arithmetic  19.5 us (4%)
  starting transfers between devices  15.7 us (3%)
  between operations  14.3 us (3%)
    psum x1, blocking collectives, local(): lax.psum(down_term(row_part, row_slots, down_cols, active_slots), 'col')  187 us
    all_gather x1, waiting for transfers between devices, local(): weight_piece = lax.all_gather(projection_weight, 'col', axis=0, tiled=True)  62.7 us
    all_gather x1, local copies, waits for them, and re-layouts, local(): weight_piece = lax.all_gather(projection_weight, 'col', axis=0, tiled=True)  51.4 us
    ppermute x1, waiting for transfers between devices, shifted(): return lax.ppermute(block, axis, route)  37.8 us
    dot_general x1, matrix products, local(): jnp.dot(own_rows, flat_piece, preferred_element_type=jnp.float32)  28.4 us
    all_gather x1, blocking collectives, local(): lax.all_gather(summed.astype(jnp.bfloat16), 'row', axis=0, tiled=True)  26.8 us
    gather x1, local copies, waits for them, and re-layouts, local(): jnp.take(page_window, pick_rows, axis=0)  16.6 us
    concatenate x2, local copies, waits for them, and re-layouts, local(): jnp.concatenate([prev_kv, own_kv, jnp.zeros((PAGE, 2, head_column_span),...  15.3 us
  transfers between devices with their start and end apart: 4, of which 2 were waited for; matrix products, arithmetic and copies ran while one was open for 16% of the time, Pallas kernels for 0%

commit v1 on v0

v1 whole, which is shorter than its diff:
```python
import jax
import jax.numpy as jnp
from jax import lax
from jax.experimental import pallas as pl
from jax.experimental.pallas import tpu as pltpu
from jax.sharding import PartitionSpec as P

HEAD_DIM = 128
PAGE = 128
SLOTS_DEV = 10
HEADS_DEV = 7
SLOTS = 16
RANK = 16
TOK = 512
WID = 448
KEEP = 640
BAND = 640

adapter_scale = 2.0
masked_score = -1e30
MESH = pl.DeviceIdType.MESH


def place():
    col = lax.axis_index("col")
    row = lax.axis_index("row")
    x, y = col // 4, col % 4
    z, k = row // 2, row % 2
    p = y // 2
    d = (k + p) % 2
    tok = x * 4 + y + d * (3 - 2 * y)
    return x, y, z, k, p, d, tok


def dev(x, y, z, k):
    return (z * 2 + k, x * 4 + y)


def fused(
    nt_ref,
    w_ref,
    at_ref,
    up_ref,
    tslot_ref,
    lo_ref,
    out_att,
    out_k,
    out_v,
    wbuf,
    nbuf,
    abuf,
    ubuf,
    raw,
    stage,
    kvwin,
    qbuf,
    att,
    acc,
    dpart,
    drecv,
    spread,
    rs,
    ss,
    ns,
    nss,
    as_,
    ass,
    ds_,
    dss,
    us,
    uss,
    raws,
    os_,
    oss,
):
    x, y, z, k, p, d, tok = place()
    xp, xm, xf = (x + 1) % 4, (x + 3) % 4, (x + 2) % 4
    zp, zm, zf = (z + 1) % 4, (z + 3) % 4, (z + 2) % 4
    mate = y + 1 - 2 * (y % 2)
    d_xp = dev(xp, y, z, k)
    d_xm = dev(xm, y, z, k)
    d_m = dev(x, mate, z, k)
    d_core = dev(x, y, z, 1 - k)
    d_swap = dev(x, 3 - y, z, 1 - k)
    d_cross = dev(x, 3 - y, z, k)
    d_zp = dev(x, y, zp, k)
    d_zm = dev(x, y, zm, k)
    b_own = (y + d) % 2
    q_own = 2 * d + b_own
    q_mate = 2 * d + 1 - b_own
    o_own = 2 * (1 - d) + (y + 1 - d) % 2
    o_mate = 2 * (1 - d) + 1 - (y + 1 - d) % 2
    lane0 = d == 0
    lane1 = d == 1
    b_src = y % 2
    xz = (x + z) % 4

    def rc(src, dst, send, recv, to):
        return pltpu.make_async_remote_copy(
            src_ref=src, dst_ref=dst, send_sem=send, recv_sem=recv, device_id=to, device_id_type=MESH
        )

    def got(ref, sem):
        rc(ref, ref, ss.at[0], sem, d_core).wait_recv()

    def sent(ref, sem):
        rc(ref, ref, sem, rs.at[0, 0], d_core).wait_send()

    def w_own(h):
        for j in range(3):
            src = w_ref.at[j, :, pl.ds(pl.multiple_of(h * HEAD_DIM, HEAD_DIM), HEAD_DIM)]
            lanes = pl.ds(j * HEAD_DIM, HEAD_DIM)

            @pl.when(lane0)
            def _():
                pltpu.make_async_copy(src, wbuf.at[h, q_own, x, :, lanes], rs.at[10, h]).start()

            @pl.when(lane1)
            def _():
                rc(src, wbuf.at[h, 2 + b_src, x, :, lanes], ss.at[10], rs.at[10, h], d_swap).start()

    for j in range(2):
        yt = y if j == 0 else mate
        xt = (x + 4 - z) % 4
        tt = xt * 4 + yt + d * (3 - 2 * yt)
        pltpu.make_async_copy(
            nt_ref.at[:, pl.ds(pl.multiple_of(tt * TOK, TOK), TOK)], raw.at[j], raws.at[j]
        ).start()
    w_own(0)
    w_own(1)

    @pl.when(tok == 0)
    def _():
        kvwin[:, 0:TOK, :] = jnp.zeros((HEADS_DEV, TOK, 2 * HEAD_DIM), jnp.bfloat16)

    for j in range(2):
        yt = y if j == 0 else mate
        xt = (x + 4 - z) % 4
        tt = xt * 4 + yt + d * (3 - 2 * yt)
        pltpu.make_async_copy(
            nt_ref.at[:, pl.ds(pl.multiple_of(tt * TOK, TOK), TOK)], raw.at[j], raws.at[j]
        ).wait()
        stage[j] = raw[j].T
        if j == 0:

            @pl.when(z == 0)
            def _():
                pltpu.make_async_copy(stage.at[0], nbuf.at[b_src, x], ns.at[b_src]).start()
                pltpu.make_async_copy(at_ref, abuf.at[b_src], as_.at[b_src]).start()

            @pl.when(z != 0)
            def _():
                rc(stage.at[0], nbuf.at[b_src, x], nss.at[0], ns.at[b_src], dev(xt, y, z, k)).start()
                rc(at_ref, abuf.at[b_src], ass.at[0], as_.at[b_src], dev(xt, y, z, k)).start()
        else:
            rc(stage.at[1], nbuf.at[b_src, x], nss.at[1], ns.at[b_src], dev(xt, mate, z, k)).start()
            rc(at_ref, abuf.at[b_src], ass.at[1], as_.at[b_src], dev(xt, mate, z, k)).start()

    @pl.when(lane0)
    def _():
        pltpu.make_async_copy(up_ref, ubuf, us).start()
        rc(up_ref, ubuf, uss, us, d_core).start()

    def down():
        for j in range(2):
            total = jnp.zeros((TOK, 2 * RANK), jnp.float32)
            for q in range(4):
                for xx in range(4):
                    first = (xx * 2 + (p + q // 2) % 2) * (2 * WID)
                    pair = abuf[j, :, pl.ds(pl.multiple_of(first, HEAD_DIM), 2 * WID)]
                    part = pair[:, (q % 2) * WID : (q % 2 + 1) * WID]
                    total = total + lax.dot_general(
                        nbuf[q, xx], part, (((1,), (1,)), ((), ())), preferred_element_type=jnp.float32
                    )
            mine = tslot_ref[...] == xz * 4 + 2 * p + j
            term = jnp.where(mine, total, 0.0).astype(jnp.bfloat16)
            dpart[0] = term if j == 0 else dpart[0] + term
        z1 = z + 1 - 2 * (z % 2)
        for s, to in enumerate((d_cross, dev(x, y, z1, k), dev(x, y, 3 - z, k))):
            rc(dpart.at[s], drecv.at[s], dss.at[s], ds_.at[s], to).start()
            got(drecv.at[s], ds_.at[s])
            dpart[s + 1] = dpart[s] + drecv[s]
        rows = lax.broadcasted_iota(jnp.int32, (2 * RANK, 2 * SLOTS * RANK), 0)
        cols = lax.broadcasted_iota(jnp.int32, (2 * RANK, 2 * SLOTS * RANK), 1)
        place_of = (rows == cols % RANK + RANK * (cols // (SLOTS * RANK))).astype(jnp.bfloat16)
        wide = jnp.dot(dpart[3], place_of, preferred_element_type=jnp.float32)
        slot_of = (lax.broadcasted_iota(jnp.int32, (TOK, 2 * SLOTS * RANK), 1) // RANK) % SLOTS
        spread[...] = jnp.where(slot_of == tslot_ref[...], wide, 0.0).astype(jnp.bfloat16)
        got(ubuf, us)

    def qkv(h):
        def part(q, carry):
            s = jnp.dot(nbuf[q, 0], wbuf[h, q, 0], preferred_element_type=jnp.float32)
            for xx in range(1, 4):
                s = s + jnp.dot(nbuf[q, xx], wbuf[h, q, xx], preferred_element_type=jnp.float32)
            acc[...] += s
            return carry

        acc[...] = jnp.zeros_like(acc)
        lax.fori_loop(0, 4, part, 0)
        lanes = pl.ds(pl.multiple_of(h * HEAD_DIM, HEAD_DIM), HEAD_DIM)
        half = SLOTS * RANK
        up_q = ubuf[:, 0, :, lanes].reshape(half, HEAD_DIM)
        up_v = ubuf[:, 1, :, lanes].reshape(half, HEAD_DIM)
        dq = jnp.dot(spread[:, :half], up_q, preferred_element_type=jnp.float32)
        dv = jnp.dot(spread[:, half:], up_v, preferred_element_type=jnp.float32)
        qbuf[h] = (acc[:, :HEAD_DIM] + adapter_scale * dq).astype(jnp.bfloat16)
        kvwin[h, TOK:, :HEAD_DIM] = acc[:, HEAD_DIM : 2 * HEAD_DIM].astype(jnp.bfloat16)
        kvwin[h, TOK:, HEAD_DIM:] = (acc[:, 2 * HEAD_DIM :] + adapter_scale * dv).astype(jnp.bfloat16)

        @pl.when(tok < 15)
        def _():
            yn, xn = (tok + 1) % 4, (tok + 1) // 4
            e = (yn // 2 + p) % 2
            rc(
                kvwin.at[h, TOK:],
                kvwin.at[h, 0:TOK],
                ss.at[11],
                rs.at[11, h],
                dev(xn, yn + e * (3 - 2 * yn), z, (p + e) % 2),
            ).start()

    def attend(h):
        @pl.when(tok > 0)
        def _():
            got(kvwin.at[h, 0:TOK], rs.at[11, h])

        def block(i, carry):
            r0 = pl.multiple_of(i * 128, 128)
            qi = qbuf[h, pl.ds(r0, 128), :]
            ki = kvwin[h, pl.ds(r0, BAND), :HEAD_DIM]
            vi = kvwin[h, pl.ds(r0, BAND), HEAD_DIM:]
            s = lax.dot_general(qi, ki, (((1,), (1,)), ((), ())), preferred_element_type=jnp.float32)
            s = s * (HEAD_DIM**-0.5)
            u = lax.broadcasted_iota(jnp.int32, (128, BAND), 1)
            r = lax.broadcasted_iota(jnp.int32, (128, BAND), 0)
            lo = lo_ref[pl.ds(r0, 128), :] - r0
            s = jnp.where((u >= lo) & (u <= r + TOK), s, masked_score)
            e = jnp.exp(s - jnp.max(s, axis=1, keepdims=True))
            total = jnp.sum(e, axis=1, keepdims=True)
            o = jnp.dot(e.astype(jnp.bfloat16), vi, preferred_element_type=jnp.float32)
            att[h, pl.ds(r0, 128), :] = (o / total).astype(jnp.bfloat16)
            return carry

        lax.fori_loop(0, 4, block, 0)
        lanes = pl.ds(pl.multiple_of(h * HEAD_DIM, HEAD_DIM), HEAD_DIM)
        moves = (
            (att.at[h], out_att.at[:, lanes]),
            (kvwin.at[h, 2 * TOK - KEEP :, 0:HEAD_DIM], out_k.at[:, lanes]),
            (kvwin.at[h, 2 * TOK - KEEP :, HEAD_DIM : 2 * HEAD_DIM], out_v.at[:, lanes]),
        )
        for n, (src, dst) in enumerate(moves):

            @pl.when(lane0)
            def _():
                pltpu.make_async_copy(src, dst, os_.at[n]).start()

            @pl.when(lane1)
            def _():
                rc(src, dst, oss.at[n], os_.at[n], d_swap).start()

    def round_(i, carry):
        @pl.when(i + 2 < HEADS_DEV)
        def _():
            w_own(i + 2)

        @pl.when(i < HEADS_DEV)
        def _():
            h = i
            own = wbuf.at[h, q_own, x]
            got(own, rs.at[10, h])
            rc(own, own, ss.at[0], rs.at[0, h], d_xp).start()
            rc(own, own, ss.at[1], rs.at[1, h], d_xm).start()
            rc(own, own, ss.at[2], rs.at[2, h], d_m).start()

        @pl.when((i >= 1) & (i < HEADS_DEV + 1))
        def _():
            h = i - 1
            got(wbuf.at[h, q_own, xm], rs.at[0, h])
            lower = wbuf.at[h, q_own, xm, 0 : WID // 2]
            rc(lower, lower, ss.at[3], rs.at[3, h], d_xp).start()
            got(wbuf.at[h, q_own, xp], rs.at[1, h])
            upper = wbuf.at[h, q_own, xp, WID // 2 : WID]
            rc(upper, upper, ss.at[4], rs.at[4, h], d_xm).start()
            other = wbuf.at[h, q_mate, x]
            got(other, rs.at[2, h])
            rc(other, other, ss.at[5], rs.at[5, h], d_xp).start()
            rc(other, other, ss.at[6], rs.at[6, h], d_xm).start()

        @pl.when((i >= 2) & (i < HEADS_DEV + 2))
        def _():
            h = i - 2
            got(wbuf.at[h, q_own, xf, 0 : WID // 2], rs.at[3, h])
            got(wbuf.at[h, q_own, xf, WID // 2 : WID], rs.at[4, h])
            far = wbuf.at[h, q_own, xf]
            rc(far, far, ss.at[7], rs.at[7, h], d_m).start()
            four = wbuf.at[h, q_own]
            rc(four, four, ss.at[8], rs.at[8, h], d_core).start()

        @pl.when((i >= 3) & (i < HEADS_DEV + 3))
        def _():
            h = i - 3
            got(wbuf.at[h, q_mate, xm], rs.at[5, h])
            got(wbuf.at[h, q_mate, xp], rs.at[6, h])
            got(wbuf.at[h, q_mate, xf], rs.at[7, h])
            four = wbuf.at[h, q_mate]
            rc(four, four, ss.at[9], rs.at[9, h], d_core).start()

        @pl.when(i == 0)
        def _():
            for b in range(2):
                got(nbuf.at[b, xz], ns.at[b])
            rc(nbuf.at[0:2, xz], nbuf.at[2:4, xz], nss.at[2], ns.at[2], d_cross).start()

        @pl.when(i == 1)
        def _():
            got(nbuf.at[2:4, xz], ns.at[2])
            rc(nbuf.at[:, xz], nbuf.at[:, xz], nss.at[3], ns.at[3], d_zp).start()
            rc(nbuf.at[:, xz], nbuf.at[:, xz], nss.at[4], ns.at[4], d_zm).start()

        @pl.when(i == 3)
        def _():
            below, above = (x + zm) % 4, (x + zp) % 4
            got(nbuf.at[:, below], ns.at[3])
            rc(nbuf.at[0:2, below], nbuf.at[0:2, below], nss.at[5], ns.at[5], d_zp).start()
            got(nbuf.at[:, above], ns.at[4])
            rc(nbuf.at[2:4, above], nbuf.at[2:4, above], nss.at[6], ns.at[6], d_zm).start()

        @pl.when(i == 5)
        def _():
            opposite = (x + zf) % 4
            got(nbuf.at[0:2, opposite], ns.at[5])
            got(nbuf.at[2:4, opposite], ns.at[6])
            for b in range(2):
                got(abuf.at[b], as_.at[b])
            down()

        @pl.when((i >= 6) & (i < HEADS_DEV + 5))
        def _():
            def one(h, c):
                attend(h)
                return c

            lax.fori_loop(i - 5 - 6 // i, i - 4, one, 0)

        @pl.when((i >= 5) & (i < HEADS_DEV + 4))
        def _():
            def one(h, c):
                got(wbuf.at[h, o_own], rs.at[8, h])
                got(wbuf.at[h, o_mate], rs.at[9, h])
                qkv(h)
                return c

            lax.fori_loop(i - 4 - 5 // i, i - 3, one, 0)

        return carry

    lax.fori_loop(0, HEADS_DEV + 5, round_, 0)

    for n in (0, 1, 2, 5, 6, 7):
        sent(wbuf.at[:, 0, 0], ss.at[n])
    for n in (3, 4):
        sent(wbuf.at[:, 0, 0, 0 : WID // 2], ss.at[n])
    for n in (8, 9):
        sent(wbuf.at[:, 0], ss.at[n])

    @pl.when(tok < 15)
    def _():
        sent(kvwin.at[:, 0:TOK], ss.at[11])

    @pl.when(z != 0)
    def _():
        sent(stage.at[0], nss.at[0])
        sent(abuf.at[0], ass.at[0])

    sent(stage.at[1], nss.at[1])
    sent(abuf.at[0], ass.at[1])
    sent(nbuf.at[0:2, 0], nss.at[2])
    sent(nbuf.at[:, 0], nss.at[3])
    sent(nbuf.at[:, 0], nss.at[4])
    sent(nbuf.at[0:2, 0], nss.at[5])
    sent(nbuf.at[0:2, 0], nss.at[6])
    for s in range(3):
        sent(dpart.at[s], dss.at[s])

    @pl.when(lane0)
    def _():
        sent(ubuf, uss)

    @pl.when(lane1)
    def _():
        sent(wbuf.at[:, 0, 0], ss.at[10])
        sent(out_att, oss.at[0])
        sent(out_k, oss.at[1])
        sent(out_v, oss.at[2])

    got(out_att, os_.at[0])
    got(out_k, os_.at[1])
    got(out_v, os_.at[2])


def run_fused(nt, w, at, up, tslot, lo):
    bf, f32 = jnp.bfloat16, jnp.float32
    dma = pltpu.SemaphoreType.DMA
    any_ = pl.BlockSpec(memory_space=pl.ANY)
    vmem = pl.BlockSpec(memory_space=pltpu.VMEM)
    wide = HEADS_DEV * HEAD_DIM
    return pl.pallas_call(
        fused,
        out_shape=(
            jax.ShapeDtypeStruct((TOK, wide), bf),
            jax.ShapeDtypeStruct((KEEP, wide), bf),
            jax.ShapeDtypeStruct((KEEP, wide), bf),
        ),
        in_specs=[any_, any_, any_, any_, vmem, vmem],
        out_specs=(any_, any_, any_),
        scratch_shapes=[
            pltpu.VMEM((HEADS_DEV, 4, 4, WID, 3 * HEAD_DIM), bf),
            pltpu.VMEM((4, 4, TOK, WID), bf),
            pltpu.VMEM((2, 2 * RANK, 16 * WID), bf),
            pltpu.VMEM((SLOTS, 2, RANK, wide), bf),
            pltpu.VMEM((2, WID, TOK), bf),
            pltpu.VMEM((2, TOK, WID), bf),
            pltpu.VMEM((HEADS_DEV, 2 * TOK, 2 * HEAD_DIM), bf),
            pltpu.VMEM((HEADS_DEV, TOK, HEAD_DIM), bf),
            pltpu.VMEM((HEADS_DEV, TOK, HEAD_DIM), bf),
            pltpu.VMEM((TOK, 3 * HEAD_DIM), f32),
            pltpu.VMEM((4, TOK, 2 * RANK), bf),
            pltpu.VMEM((3, TOK, 2 * RANK), bf),
            pltpu.VMEM((TOK, 2 * SLOTS * RANK), bf),
            dma((12, HEADS_DEV)),
            dma((12,)),
            dma((7,)),
            dma((7,)),
            dma((2,)),
            dma((2,)),
            dma((3,)),
            dma((3,)),
            dma,
            dma,
            dma((2,)),
            dma((3,)),
            dma((3,)),
        ],
        compiler_params=pltpu.CompilerParams(has_side_effects=True, vmem_limit_bytes=67_043_328),
    )(nt, w, at, up, tslot, lo)


def local(
    normed,
    projection_weight,
    adapter_down_weight,
    adapter_up_weight,
    packed_prompt_length,
    prompt_adapter_ids,
    slot_adapter_ids,
    prompt_page_slots,
):
    col = lax.axis_index("col")
    tok = place()[-1]
    ends = jnp.cumsum(packed_prompt_length)
    starts = ends - packed_prompt_length
    matched = slot_adapter_ids[None, :] == prompt_adapter_ids[:, None]
    slot_of = jnp.sum(jnp.where(matched, jnp.arange(SLOTS, dtype=jnp.int32)[None, :], 0), axis=1)
    positions = tok * TOK + jnp.arange(TOK, dtype=jnp.int32)
    inside = (positions[:, None] >= starts[None, :]) & (positions[:, None] < ends[None, :])
    tslot = jnp.sum(jnp.where(inside, slot_of[None, :], 0), axis=1, keepdims=True)
    first = jnp.sum(jnp.where(inside, starts[None, :], 0), axis=1, keepdims=True)
    lo = first - (tok * TOK - TOK)
    attended, keys, values = run_fused(
        normed.T,
        jnp.transpose(projection_weight, (1, 0, 2)),
        jnp.transpose(adapter_down_weight, (1, 2, 0))[0],
        adapter_up_weight,
        tslot,
        lo,
    )
    window = jnp.pad(jnp.stack([keys, values], axis=1), ((0, PAGE), (0, 0), (0, 0)))
    pages = prompt_page_slots.shape[1]
    page_index = jnp.arange(pages, dtype=jnp.int32)
    page_rows = jnp.clip(packed_prompt_length[:, None] - PAGE * page_index[None, :], 0, PAGE)
    page_first = starts[:, None] + PAGE * page_index[None, :]
    my_slots = col * SLOTS_DEV + jnp.arange(SLOTS_DEV, dtype=jnp.int32)
    hit = prompt_page_slots.reshape(-1)[None, :] == my_slots[:, None]
    used = jnp.sum(jnp.where(hit, page_rows.reshape(-1)[None, :], 0), axis=1)
    first_used = jnp.sum(jnp.where(hit, page_first.reshape(-1)[None, :], 0), axis=1)
    offset = jnp.clip(first_used - (col * TOK + TOK - KEEP), 0, KEEP)
    lines = jnp.arange(PAGE, dtype=jnp.int32)
    out = []
    for i in range(SLOTS_DEV):
        rows = lax.dynamic_slice_in_dim(window, offset[i], PAGE, 0)
        out.append(jnp.where((lines < used[i])[:, None, None], rows, jnp.zeros_like(rows)))
    return attended, jnp.stack(out)


def solution(mesh):
    placed = (
        P(None, "col"),
        P("col", None, "row"),
        P(None, "col", None),
        P(None, None, None, "row"),
        P(),
        P(),
        P(),
        P(),
    )
    return jax.shard_map(
        local,
        mesh=mesh,
        in_specs=placed,
        out_specs=(P("col", "row"), P("col", None, None, "row")),
        check_vma=False,
    )
```

time: 547 us -> 312 us (0.57); the launches traced: 537 us -> 309 us
  Pallas kernels: 0 us -> 249 us
  blocking collectives: 213 us -> 0 us
  local copies, waits for them, and re-layouts: 121 us -> 15.2 us
  waiting for transfers between devices: 101 us -> 0 us
  matrix products: 52.6 us -> 0 us
  starting transfers between devices: 15.7 us -> 0 us
  other arithmetic: 19.5 us -> 25.8 us
    pallas_call x0 -> x1, Pallas kernels: none -> 249 us  [run_fused(): pl.pallas_call(fused, out_shape=(jax.ShapeDtypeStruct((TOK, wide), bf), j...]
    psum x1 -> x0, blocking collectives: 187 us -> none  [local(): lax.psum(down_term(row_part, row_slots, down_cols, active_slots), 'col')]
    all_gather x1 -> x0, waiting for transfers between devices: 62.7 us -> none  [local(): weight_piece = lax.all_gather(projection_weight, 'col', axis=0, tiled=True)]
    all_gather x1 -> x0, local copies, waits for them, and re-layouts: 51.4 us -> none  [local(): weight_piece = lax.all_gather(projection_weight, 'col', axis=0, tiled=True)]
    dot_general x5 -> x0, matrix products: 39.9 us -> none  [the longest x1 28.4 us: local(): jnp.dot(own_rows, flat_piece, preferred_element_type=jnp.float32)]
    ppermute x1 -> x0, waiting for transfers between devices: 37.8 us -> none  [shifted(): return lax.ppermute(block, axis, route)]
    all_gather x1 -> x0, blocking collectives: 26.8 us -> none  [local(): lax.all_gather(summed.astype(jnp.bfloat16), 'row', axis=0, tiled=True)]
    gather x1 -> x0, local copies, waits for them, and re-layouts: 16.6 us -> none  [local(): jnp.take(page_window, pick_rows, axis=0)]
  transfers between devices with their start and end apart: 4 -> 0, of which waited for: 2 -> 0; matrix products, arithmetic and copies ran while one was open for 16% -> 0% of each run, Pallas kernels for 0% -> 0%
where the time goes in v1:
time: 312 us; the launch traced here: 309 us
  Pallas kernels  249 us (80%)
  other arithmetic  25.8 us (8%)
  between operations  19.7 us (6%)
  local copies, waits for them, and re-layouts  15.2 us (5%)
    pallas_call x1, Pallas kernels, run_fused(): pl.pallas_call(fused, out_shape=(jax.ShapeDtypeStruct((TOK, wide), bf), j...  249 us
    lt x10, other arithmetic, local(): lines < used[i]  11.8 us
    unnamed x25, local copies, waits for them, and re-layouts  11 us
    unnamed x9, other arithmetic  8.59 us

profile of v1, /device:TPU:3, one launch (start us, length us, event | category | flops | bytes accessed | tf_op | source)
XLA Modules:
  0.0 309.3 jit_solution(5993861271688492732)
XLA Ops:
  0.7 0.8 select_reduce_fusion.2
  1.5 0.8 copy.20
  2.3 0.1 eq.35
  2.4 0.7 copy.17
  3.1 0.1 reduce-window.8
  3.2 0.1 reduce
  3.3 0.7 sub.56
  4.0 0.1 select_reduce_fusion
  4.1 0.7 broadcast_add_fusion
  4.9 0.1 add.108
  5.0 0.1 min.20
  5.1 0.2 fusion.3
  5.3 0.7 fusion.6
  24.8 0.7 fusion.5
  25.5 1.1 iota_compare_fusion.1
  26.6 1.2 iota_compare_fusion.2
  27.9 1.2 iota_compare_fusion.3
  29.1 1.1 iota_compare_fusion.4
  30.2 1.2 iota_compare_fusion.5
  31.4 1.1 iota_compare_fusion.6
  32.5 1.2 iota_compare_fusion.7
  33.7 1.2 iota_compare_fusion.8
  34.9 1.1 iota_compare_fusion.9
  36.0 1.3 iota_compare_fusion.10
  37.3 0.9 copy.18.tslot_ref
  38.2 0.9 copy.19.lo_ref
  39.0 248.5 %shard_map.95 = (bf16[512,896]{1,0:T(8,128)(2,1)}, bf16[640,896]{1,0:T(8,128)(2,1)}, bf16[640,896]{1,0:T(8,128)(2,1)}) custom-call(bf16[448,8192]{1,0:T(8,128)(2,1)} %bitcast.50, bf16[3,448,896]{2,1,0:T(8,128)(2,1)} %bitcast.51, bf16[32,7168]{1,0:T(8,128)(2,1)} %bitcast.54, bf16[16,2,16,896]{3,2,1,0:T(8,128)(2,1)} %up_ref.1, s32[512,1]{1,0:T(8,128)} %copy.18.tslot_ref, ...), custom_call_target="tpu_custom_call" | custom-call | tf_op jit(solution)/shard_map/pallas_call | solution.py:408
  287.6 0.0 copy-start.10
  287.6 0.0 copy-start.9
  287.6 0.0 copy-start.8
  287.6 1.8 fusion.2
  289.5 0.0 copy-done.10
  289.5 0.0 copy-start.2
  289.5 0.0 copy-start.1
  289.5 0.9 bitcast_dynamic-update-slice_fusion.9
  290.4 1.0 bitcast_dynamic-update-slice_fusion.8
  291.4 0.0 copy-done.8
  291.4 1.0 bitcast_dynamic-update-slice_fusion.7
  292.4 1.0 bitcast_dynamic-update-slice_fusion.6
  293.3 1.0 bitcast_dynamic-update-slice_fusion.5
  294.3 0.0 copy-done.5
  294.3 0.9 bitcast_dynamic-update-slice_fusion.4
  295.2 1.0 bitcast_dynamic-update-slice_fusion.3
  296.2 0.9 bitcast_dynamic-update-slice_fusion.2
  297.2 1.0 bitcast_dynamic-update-slice_fusion.1
  298.1 0.9 bitcast_dynamic-update-slice_fusion
  299.1 9.3 %copy.21 = bf16[10,128,2,896]{3,2,1,0:T(2,128)(2,1)} copy(bf16[10,128,2,896]{3,1,2,0:T(8,128)(2,1)} %bitcast_dynamic-update-slice_fusion) | data formatting | bytes 9175040
  308.3 0.9 copy.32
  (19 shorter events, 0.1 us)
Async XLA Ops:
  287.6 1.9 copy-start.10
  287.6 2.9 copy-start.9
  287.6 3.8 %copy-start.8 = (pred[128]{0:T(512)(128)(4,1)S(1)}, pred[128]{0:T(512)(128)(4,1)}, u32[]{:S(2)}) copy-start(pred[128]{0:T(512)(128)(4,1)} %iota_compare_fusion.8) | copy-start | bytes 388
  287.6 4.8 %copy-start.7 = (pred[128]{0:T(512)(128)(4,1)S(1)}, pred[128]{0:T(512)(128)(4,1)}, u32[]{:S(2)}) copy-start(pred[128]{0:T(512)(128)(4,1)} %iota_compare_fusion.7) | copy-start | bytes 388
  287.6 5.7 %copy-start.6 = (pred[128]{0:T(512)(128)(4,1)S(1)}, pred[128]{0:T(512)(128)(4,1)}, u32[]{:S(2)}) copy-start(pred[128]{0:T(512)(128)(4,1)} %iota_compare_fusion.6) | copy-start | bytes 388
  287.6 6.7 %copy-start.5 = (pred[128]{0:T(512)(128)(4,1)S(1)}, pred[128]{0:T(512)(128)(4,1)}, u32[]{:S(2)}) copy-start(pred[128]{0:T(512)(128)(4,1)} %iota_compare_fusion.5) | copy-start | bytes 388
  287.6 7.6 %copy-start.4 = (pred[128]{0:T(512)(128)(4,1)S(1)}, pred[128]{0:T(512)(128)(4,1)}, u32[]{:S(2)}) copy-start(pred[128]{0:T(512)(128)(4,1)} %iota_compare_fusion.4) | copy-start | bytes 388
  287.6 8.6 %copy-start.3 = (pred[128]{0:T(512)(128)(4,1)S(1)}, pred[128]{0:T(512)(128)(4,1)}, u32[]{:S(2)}) copy-start(pred[128]{0:T(512)(128)(4,1)} %iota_compare_fusion.3) | copy-start | bytes 388
  289.5 7.7 %copy-start.2 = (pred[128]{0:T(512)(128)(4,1)S(1)}, pred[128]{0:T(512)(128)(4,1)}, u32[]{:S(2)}) copy-start(pred[128]{0:T(512)(128)(4,1)} %iota_compare_fusion.2) | copy-start | bytes 388
  289.5 8.6 %copy-start.1 = (pred[128]{0:T(512)(128)(4,1)S(1)}, pred[128]{0:T(512)(128)(4,1)}, u32[]{:S(2)}) copy-start(pred[128]{0:T(512)(128)(4,1)} %iota_compare_fusion.1) | copy-start | bytes 388
  299.1 9.3 %copy-start = (bf16[512,896]{1,0:T(8,128)(2,1)S(1)}, bf16[512,896]{1,0:T(8,128)(2,1)}, u32[]{:S(2)}) copy-start(bf16[512,896]{1,0:T(8,128)(2,1)} %get-tuple-element.42) | copy-start | bytes 2752516

commit v2 on v1

v2 whole, which is shorter than its diff:
```python
import jax
import jax.numpy as jnp
from jax import lax
from jax.experimental import pallas as pl
from jax.experimental.pallas import tpu as pltpu
from jax.sharding import PartitionSpec as P

HEAD_DIM = 128
PAGE = 128
SLOTS_DEV = 10
HEADS_DEV = 7
SLOTS = 16
RANK = 16
TOK = 512
WID = 448
KEEP = 640
BAND = 640
PROMPTS = 64
QUARTER = 128
FAR = 128
VIA = 400

adapter_scale = 2.0
masked_score = -1e30
MESH = pl.DeviceIdType.MESH


def place():
    col = lax.axis_index("col")
    row = lax.axis_index("row")
    x, y = col // 4, col % 4
    z, k = row // 2, row % 2
    p = y // 2
    d = (k + p) % 2
    tok = x * 4 + y + d * (3 - 2 * y)
    return x, y, z, k, p, d, tok


def dev(x, y, z, k):
    return (z * 2 + k, x * 4 + y)


def holder(t, z, p):
    x, y = t // 4, t % 4
    e = (y // 2 + p) % 2
    return dev(x, y + e * (3 - 2 * y), z, (p + e) % 2)


def to_column(line, n):
    r = lax.broadcasted_iota(jnp.int32, (n, n), 0)
    c = lax.broadcasted_iota(jnp.int32, (n, n), 1)
    return jnp.sum(jnp.where(r == c, line, 0.0), axis=1, keepdims=True)


def fused(
    nt_ref,
    w_ref,
    at_ref,
    up_ref,
    len_ref,
    ask_ref,
    slot_ref,
    page_ref,
    out_att,
    out_k,
    out_v,
    out_page,
    wbuf,
    nbuf,
    abuf,
    ubuf,
    raw,
    stage,
    kvwin,
    qbuf,
    att,
    acc,
    dpart,
    drecv,
    spread,
    tslot,
    low,
    rs,
    ss,
    ns,
    nss,
    as_,
    ass,
    ds_,
    dss,
    us,
    uss,
    raws,
    os_,
    oss,
):
    x, y, z, k, p, d, tok = place()
    xp, xm, xf = (x + 1) % 4, (x + 3) % 4, (x + 2) % 4
    zp, zm, zf = (z + 1) % 4, (z + 3) % 4, (z + 2) % 4
    mate = y + 1 - 2 * (y % 2)
    d_xp = dev(xp, y, z, k)
    d_xm = dev(xm, y, z, k)
    d_m = dev(x, mate, z, k)
    d_core = dev(x, y, z, 1 - k)
    d_swap = dev(x, 3 - y, z, 1 - k)
    d_cross = dev(x, 3 - y, z, k)
    d_zp = dev(x, y, zp, k)
    d_zm = dev(x, y, zm, k)
    b_own = (y + d) % 2
    q_own = 2 * d + b_own
    q_mate = 2 * d + 1 - b_own
    o_own = 2 * (1 - d) + (y + 1 - d) % 2
    o_mate = 2 * (1 - d) + 1 - (y + 1 - d) % 2
    lane0 = d == 0
    lane1 = d == 1
    b_src = y % 2

    def rc(src, dst, send, recv, to):
        return pltpu.make_async_remote_copy(
            src_ref=src, dst_ref=dst, send_sem=send, recv_sem=recv, device_id=to, device_id_type=MESH
        )

    def got(ref, sem):
        rc(ref, ref, ss.at[0], sem, d_core).wait_recv()

    def sent(ref, sem):
        rc(ref, ref, sem, rs.at[0, 0], d_core).wait_send()

    barrier = pltpu.get_barrier_semaphore()

    def greet(to):
        pl.semaphore_signal(barrier, inc=1, device_id=to, device_id_type=MESH)

    near = [d_core, d_swap, d_cross, d_zp, d_zm, d_m]
    for xt in (xp, xm, xf):
        near += [dev(xt, y, z, k), dev(xt, mate, z, k)]
    for to in near:
        greet(to)

    greet(holder((tok + 1) % 16, z, p))
    greet(holder((tok + 15) % 16, z, p))
    pl.semaphore_wait(barrier, len(near) + 2)

    def w_own(h):
        for j in range(3):
            src = w_ref.at[j, :, pl.ds(pl.multiple_of(h * HEAD_DIM, HEAD_DIM), HEAD_DIM)]
            lanes = pl.ds(j * HEAD_DIM, HEAD_DIM)

            @pl.when(lane0)
            def _():
                pltpu.make_async_copy(src, wbuf.at[h, q_own, x, :, lanes], rs.at[10, h]).start()

            @pl.when(lane1)
            def _():
                rc(src, wbuf.at[h, 2 + b_src, x, :, lanes], ss.at[10], rs.at[10, h], d_swap).start()

    def w_first(h):
        own = wbuf.at[h, q_own, x]
        got(own, rs.at[10, h])
        rc(own, own, ss.at[0], rs.at[0, h], d_xp).start()
        rc(own, own, ss.at[1], rs.at[1, h], d_xm).start()
        rc(own, own, ss.at[2], rs.at[2, h], d_m).start()

    def block_of(n):
        xt = n // 2
        yt = y + (n % 2) * (mate - y)
        tt = xt * 4 + yt + d * (3 - 2 * yt)
        first = pl.multiple_of(tt * TOK + z * QUARTER, QUARTER)
        return xt, yt, pltpu.make_async_copy(
            nt_ref.at[:, pl.ds(first, QUARTER)], raw.at[n], raws.at[n]
        )

    def load(n, c):
        block_of(n)[2].start()
        return c

    lax.fori_loop(0, 8, load, 0)
    w_own(0)
    w_own(1)
    w_own(2)
    mine = pl.ds(pl.multiple_of(z * QUARTER, QUARTER), QUARTER)
    ranks = pl.ds(pl.multiple_of(z * 8, 8), 8)

    def scatter(n, c):
        xt, yt, copy = block_of(n)
        copy.wait()
        stage[n] = raw[n].T
        itself = (xt == x) & (n % 2 == 0)

        @pl.when(itself)
        def _():
            pltpu.make_async_copy(stage.at[n], nbuf.at[b_src, x, mine], ns.at[0]).start()

        @pl.when(jnp.logical_not(itself))
        def _():
            rc(stage.at[n], nbuf.at[b_src, x, mine], nss.at[0], ns.at[0], dev(xt, yt, z, k)).start()

        @pl.when((b_src == k) & itself)
        def _():
            pltpu.make_async_copy(at_ref.at[ranks], abuf.at[b_src, x], as_.at[0]).start()

        @pl.when((b_src == k) & jnp.logical_not(itself))
        def _():
            rc(at_ref.at[ranks], abuf.at[b_src, x], ass.at[0], as_.at[0], dev(xt, yt, z, k)).start()

        return c

    @pl.when(lane0)
    def _():
        w_first(0)

    lax.fori_loop(0, 8, scatter, 0)

    @pl.when(lane1)
    def _():
        w_first(0)

    @pl.when(lane0)
    def _():
        pltpu.make_async_copy(up_ref, ubuf, us).start()
        rc(up_ref, ubuf, uss, us, d_core).start()

    @pl.when(tok == 0)
    def _():
        kvwin[:, 0:TOK, :] = jnp.zeros((HEADS_DEV, TOK, 2 * HEAD_DIM), jnp.bfloat16)

    f32 = jnp.float32
    lens = len_ref[...].astype(f32)
    r64 = lax.broadcasted_iota(jnp.int32, (PROMPTS, PROMPTS), 0)
    c64 = lax.broadcasted_iota(jnp.int32, (PROMPTS, PROMPTS), 1)
    starts = jnp.sum(jnp.where(r64 < c64, to_column(lens, PROMPTS), 0.0), axis=0, keepdims=True)
    slot_col = to_column(slot_ref[...].astype(f32), SLOTS)
    s_row = lax.broadcasted_iota(jnp.int32, (SLOTS, PROMPTS), 0)
    slot_of = jnp.sum(
        jnp.where(slot_col == ask_ref[...].astype(f32), s_row.astype(f32), 0.0), axis=0, keepdims=True
    )
    at = (lax.broadcasted_iota(jnp.int32, (TOK, PROMPTS), 0) + tok * TOK).astype(f32)
    inside = (at >= starts) & (at < starts + lens)
    tslot[...] = jnp.sum(jnp.where(inside, slot_of, 0.0), axis=1, keepdims=True).astype(jnp.int32)
    first = jnp.sum(jnp.where(inside, starts, 0.0), axis=1, keepdims=True).astype(jnp.int32)
    low[...] = first - (tok - 1) * TOK
    my_col = x * 4 + y
    where_ = s_row + my_col * SLOTS_DEV
    offset = jnp.zeros((SLOTS, 1), f32)
    used = jnp.zeros((SLOTS, 1), f32)
    for j in range(page_ref.shape[0]):
        hit = page_ref[j : j + 1, :] == where_
        offset += jnp.sum(jnp.where(hit, starts + float(PAGE * j), 0.0), axis=1, keepdims=True)
        used += jnp.sum(
            jnp.where(hit, jnp.clip(lens - float(PAGE * j), 0.0, float(PAGE)), 0.0), axis=1, keepdims=True
        )
    base = my_col * TOK + TOK - KEEP
    offset = jnp.clip(offset.astype(jnp.int32) - base, 0, KEEP - 1)
    lane = lax.broadcasted_iota(jnp.int32, (SLOTS, 128), 1)
    out_page[...] = jnp.where(lane == 0, offset, used.astype(jnp.int32))

    def down():
        total = jnp.zeros((TOK, 64), f32)
        for q in range(4):
            for xx in range(4):
                begin = (xx * 2 + (p + q // 2) % 2) * (2 * WID)
                pair = abuf[:, :, :, pl.ds(pl.multiple_of(begin, HEAD_DIM), 2 * WID)].reshape(64, 2 * WID)
                part = pair[:, (q % 2) * WID : (q % 2 + 1) * WID]
                total = total + lax.dot_general(
                    nbuf[q, xx], part, (((1,), (1,)), ((), ())), preferred_element_type=f32
                )
        n = lax.broadcasted_iota(jnp.int32, (TOK, 64), 1)
        slot = ((n // 8) % 4) * 4 + 2 * p + n // 32
        term = jnp.where(slot == tslot[...], total, 0.0).astype(jnp.bfloat16)
        rows = lax.broadcasted_iota(jnp.int32, (64, 2 * RANK), 0)
        cols = lax.broadcasted_iota(jnp.int32, (64, 2 * RANK), 1)
        fold = (cols == rows % 8 + 8 * z).astype(jnp.bfloat16)
        dpart[0] = jnp.dot(term, fold, preferred_element_type=f32).astype(jnp.bfloat16)
        z1 = z + 1 - 2 * (z % 2)
        for s, to in enumerate((d_cross, dev(x, y, z1, k), dev(x, y, 3 - z, k))):
            rc(dpart.at[s], drecv.at[s], dss.at[s], ds_.at[s], to).start()
            got(drecv.at[s], ds_.at[s])
            dpart[s + 1] = dpart[s] + drecv[s]
        rows = lax.broadcasted_iota(jnp.int32, (2 * RANK, 2 * SLOTS * RANK), 0)
        cols = lax.broadcasted_iota(jnp.int32, (2 * RANK, 2 * SLOTS * RANK), 1)
        place_of = (rows == cols % RANK + RANK * (cols // (SLOTS * RANK))).astype(jnp.bfloat16)
        wide = jnp.dot(dpart[3], place_of, preferred_element_type=f32)
        slot_at = (lax.broadcasted_iota(jnp.int32, (TOK, 2 * SLOTS * RANK), 1) // RANK) % SLOTS
        spread[...] = jnp.where(slot_at == tslot[...], wide, 0.0).astype(jnp.bfloat16)
        got(ubuf, us)

    def head_lanes(h):
        return pl.ds(pl.multiple_of(h * HEAD_DIM, HEAD_DIM), HEAD_DIM)

    def deliver(moves):
        for src, dst, n in moves:

            @pl.when(lane0)
            def _():
                pltpu.make_async_copy(src, dst, os_.at[n]).start()

            @pl.when(lane1)
            def _():
                rc(src, dst, oss.at[n], os_.at[n], d_swap).start()

    def qkv(h, n):
        def part(q):
            s = jnp.dot(nbuf[q, 0], wbuf[h, q, 0], preferred_element_type=f32)
            for xx in range(1, 4):
                s = s + jnp.dot(nbuf[q, xx], wbuf[h, q, xx], preferred_element_type=f32)
            acc[...] += s

        def theirs(own):
            return own * o_own + (1 - own) * o_mate

        @pl.when(n == 0)
        def _():
            acc[...] = jnp.zeros_like(acc)

        part((1 - n) * q_own + n * q_mate)
        got(wbuf.at[h, theirs(1 - n)], rs.at[8 + n, h])
        part(theirs(1 - n))

        @pl.when(n == 1)
        def _():
            finish(h)

    def finish(h):
        lanes = pl.ds(pl.multiple_of(h * HEAD_DIM, HEAD_DIM), HEAD_DIM)
        half = SLOTS * RANK
        up_q = ubuf[:, 0, :, lanes].reshape(half, HEAD_DIM)
        up_v = ubuf[:, 1, :, lanes].reshape(half, HEAD_DIM)
        dq = jnp.dot(spread[:, :half], up_q, preferred_element_type=f32)
        dv = jnp.dot(spread[:, half:], up_v, preferred_element_type=f32)
        qbuf[h] = (acc[:, :HEAD_DIM] + adapter_scale * dq).astype(jnp.bfloat16)
        kvwin[h, TOK:, :HEAD_DIM] = acc[:, HEAD_DIM : 2 * HEAD_DIM].astype(jnp.bfloat16)
        kvwin[h, TOK:, HEAD_DIM:] = (acc[:, 2 * HEAD_DIM :] + adapter_scale * dv).astype(jnp.bfloat16)

        @pl.when(tok < 15)
        def _():
            rc(
                kvwin.at[h, TOK:], kvwin.at[h, 0:TOK], ss.at[11], rs.at[11, h], holder(tok + 1, z, p)
            ).start()

        deliver(
            (
                (kvwin.at[h, TOK:, 0:HEAD_DIM], out_k.at[KEEP - TOK :, head_lanes(h)], 1),
                (kvwin.at[h, TOK:, HEAD_DIM:], out_v.at[KEEP - TOK :, head_lanes(h)], 2),
            )
        )

    def attend(h):
        @pl.when(tok > 0)
        def _():
            got(kvwin.at[h, 0:TOK], rs.at[11, h])

        def block(i, carry):
            r0 = pl.multiple_of(i * 128, 128)
            qi = qbuf[h, pl.ds(r0, 128), :]
            ki = kvwin[h, pl.ds(r0, BAND), :HEAD_DIM]
            vi = kvwin[h, pl.ds(r0, BAND), HEAD_DIM:]
            s = lax.dot_general(qi, ki, (((1,), (1,)), ((), ())), preferred_element_type=f32)
            s = s * (HEAD_DIM**-0.5)
            u = lax.broadcasted_iota(jnp.int32, (128, BAND), 1)
            r = lax.broadcasted_iota(jnp.int32, (128, BAND), 0)
            lo = low[pl.ds(r0, 128), :] - r0
            s = jnp.where((u >= lo) & (u <= r + TOK), s, masked_score)
            e = jnp.exp(s - jnp.max(s, axis=1, keepdims=True))
            total = jnp.sum(e, axis=1, keepdims=True)
            o = jnp.dot(e.astype(jnp.bfloat16), vi, preferred_element_type=f32)
            att[h, pl.ds(r0, 128), :] = (o / total).astype(jnp.bfloat16)
            return carry

        early = pl.ds(2 * TOK - KEEP, KEEP - TOK)
        deliver(
            (
                (kvwin.at[h, early, 0:HEAD_DIM], out_k.at[0 : KEEP - TOK, head_lanes(h)], 1),
                (kvwin.at[h, early, HEAD_DIM:], out_v.at[0 : KEEP - TOK, head_lanes(h)], 2),
            )
        )
        lax.fori_loop(0, 4, block, 0)
        deliver(((att.at[h], out_att.at[:, head_lanes(h)], 0),))

    def tokens_of(zz):
        return pl.ds(pl.multiple_of(zz * QUARTER, QUARTER), QUARTER)

    def round_(i, carry):
        @pl.when(i + 3 < HEADS_DEV)
        def _():
            w_own(i + 3)

        @pl.when(i + 1 < HEADS_DEV)
        def _():
            w_first(i + 1)

        @pl.when(i < HEADS_DEV)
        def _():
            h = i
            got(wbuf.at[h, q_own, xm], rs.at[0, h])
            lower = wbuf.at[h, q_own, xm, 0:FAR]
            rc(lower, lower, ss.at[3], rs.at[3, h], d_xp).start()
            rest = wbuf.at[h, q_own, xm, VIA:WID]
            rc(rest, rest, ss.at[12], rs.at[12, h], d_m).start()
            got(wbuf.at[h, q_own, xp], rs.at[1, h])
            upper = wbuf.at[h, q_own, xp, FAR:WID]
            rc(upper, upper, ss.at[4], rs.at[4, h], d_xm).start()
            rest = wbuf.at[h, q_own, xp, VIA:WID]
            rc(rest, rest, ss.at[13], rs.at[13, h], d_m).start()
            got(wbuf.at[h, q_mate, x], rs.at[2, h])
            other = wbuf.at[h, q_mate, x, 0:VIA]
            rc(other, other, ss.at[5], rs.at[5, h], d_xp).start()
            rc(other, other, ss.at[6], rs.at[6, h], d_xm).start()

        @pl.when((i >= 1) & (i < HEADS_DEV + 1))
        def _():
            h = i - 1
            got(wbuf.at[h, q_own, xf, 0:FAR], rs.at[3, h])
            got(wbuf.at[h, q_own, xf, FAR:WID], rs.at[4, h])
            far = wbuf.at[h, q_own, xf]
            rc(far, far, ss.at[7], rs.at[7, h], d_m).start()
            four = wbuf.at[h, q_own]
            rc(four, four, ss.at[8], rs.at[8, h], d_core).start()

        @pl.when(i == 0)
        def _():
            got(nbuf.at[0:2, :, mine], ns.at[0])
            u = nbuf.at[0:2, :, mine]
            rc(u, nbuf.at[2:4, :, mine], nss.at[1], ns.at[1], d_cross).start()
            rc(u, u, nss.at[2], ns.at[2], d_zp).start()
            rc(u, u, nss.at[3], ns.at[3], d_zm).start()
            got(abuf.at[k], as_.at[0])
            rc(abuf.at[k], abuf.at[k], ass.at[1], as_.at[1], d_core).start()

        @pl.when(i == 2)
        def _():
            u = nbuf.at[2:4, :, mine]
            got(u, ns.at[1])
            rc(u, u, nss.at[4], ns.at[4], d_zp).start()
            rc(u, u, nss.at[5], ns.at[5], d_zm).start()
            got(nbuf.at[0:2, :, tokens_of(zm)], ns.at[2])
            u = nbuf.at[0, :, tokens_of(zm)]
            rc(u, u, nss.at[6], ns.at[6], d_zp).start()
            got(nbuf.at[0:2, :, tokens_of(zp)], ns.at[3])
            u = nbuf.at[1, :, tokens_of(zp)]
            rc(u, u, nss.at[7], ns.at[7], d_zm).start()

        @pl.when(i == 3)
        def _():
            got(nbuf.at[2:4, :, tokens_of(zm)], ns.at[4])
            u = nbuf.at[2, :, tokens_of(zm)]
            rc(u, u, nss.at[8], ns.at[8], d_zp).start()
            got(nbuf.at[2:4, :, tokens_of(zp)], ns.at[5])
            u = nbuf.at[3, :, tokens_of(zp)]
            rc(u, u, nss.at[9], ns.at[9], d_zm).start()

        @pl.when(i == 4)
        def _():
            for q in range(4):
                got(nbuf.at[q, :, tokens_of(zf)], ns.at[6 + q])
            got(abuf.at[1 - k], as_.at[1])
            down()

        @pl.when(i >= 5)
        def _():
            def one(h, c):
                attend(h)
                return c

            lax.fori_loop(i - 4 - 6 // i, i - 3 - 6 // (i + 1), one, 0)

        def first_step(i):
            return 2 * i - 5 - 6 // i - 2 * (5 // i)

        @pl.when((i >= 4) & (i < HEADS_DEV + 3))
        def _():
            def one(step, c):
                @pl.when(step < 2 * HEADS_DEV)
                def _():
                    qkv(step // 2, step % 2)

                return c

            lax.fori_loop(first_step(i), first_step(i + 1), one, 0)

        @pl.when((i >= 2) & (i < HEADS_DEV + 2))
        def _():
            h = i - 2
            got(wbuf.at[h, q_mate, xm, 0:VIA], rs.at[5, h])
            got(wbuf.at[h, q_mate, xp, 0:VIA], rs.at[6, h])
            got(wbuf.at[h, q_mate, xm, VIA:WID], rs.at[12, h])
            got(wbuf.at[h, q_mate, xp, VIA:WID], rs.at[13, h])
            got(wbuf.at[h, q_mate, xf], rs.at[7, h])
            four = wbuf.at[h, q_mate]
            rc(four, four, ss.at[9], rs.at[9, h], d_core).start()

        return carry

    lax.fori_loop(0, HEADS_DEV + 4, round_, 0)

    for n in (0, 1, 2, 7):
        sent(wbuf.at[:, 0, 0], ss.at[n])
    sent(wbuf.at[:, 0, 0, 0:FAR], ss.at[3])
    sent(wbuf.at[:, 0, 0, FAR:WID], ss.at[4])
    for n in (5, 6):
        sent(wbuf.at[:, 0, 0, 0:VIA], ss.at[n])
    for n in (12, 13):
        sent(wbuf.at[:, 0, 0, VIA:WID], ss.at[n])
    for n in (8, 9):
        sent(wbuf.at[:, 0], ss.at[n])

    @pl.when(tok < 15)
    def _():
        sent(kvwin.at[:, 0:TOK], ss.at[11])

    sent(stage.at[0:7], nss.at[0])
    for n in range(1, 6):
        sent(nbuf.at[0:2, :, mine], nss.at[n])
    for n in range(6, 10):
        sent(nbuf.at[0, :, mine], nss.at[n])

    @pl.when(b_src == k)
    def _():
        sent(w_ref.at[0], ass.at[0])

    sent(abuf.at[0], ass.at[1])
    for s in range(3):
        sent(dpart.at[s], dss.at[s])

    @pl.when(lane0)
    def _():
        sent(ubuf, uss)

    @pl.when(lane1)
    def _():
        sent(wbuf.at[:, 0, 0], ss.at[10])
        sent(out_att, oss.at[0])
        sent(out_k, oss.at[1])
        sent(out_v, oss.at[2])

    got(out_att, os_.at[0])
    got(out_k, os_.at[1])
    got(out_v, os_.at[2])


def run_fused(*operands):
    bf, f32, i32 = jnp.bfloat16, jnp.float32, jnp.int32
    dma = pltpu.SemaphoreType.DMA
    any_ = pl.BlockSpec(memory_space=pl.ANY)
    vmem = pl.BlockSpec(memory_space=pltpu.VMEM)
    wide = HEADS_DEV * HEAD_DIM
    return pl.pallas_call(
        fused,
        out_shape=(
            jax.ShapeDtypeStruct((TOK, wide), bf),
            jax.ShapeDtypeStruct((KEEP, wide), bf),
            jax.ShapeDtypeStruct((KEEP, wide), bf),
            jax.ShapeDtypeStruct((SLOTS, 128), i32),
        ),
        in_specs=[any_] * 4 + [vmem] * 4,
        out_specs=(any_, any_, any_, vmem),
        scratch_shapes=[
            pltpu.VMEM((HEADS_DEV, 4, 4, WID, 3 * HEAD_DIM), bf),
            pltpu.VMEM((4, 4, TOK, WID), bf),
            pltpu.VMEM((2, 4, 8, 16 * WID), bf),
            pltpu.VMEM((SLOTS, 2, RANK, wide), bf),
            pltpu.VMEM((8, WID, QUARTER), bf),
            pltpu.VMEM((8, QUARTER, WID), bf),
            pltpu.VMEM((HEADS_DEV, 2 * TOK, 2 * HEAD_DIM), bf),
            pltpu.VMEM((HEADS_DEV, TOK, HEAD_DIM), bf),
            pltpu.VMEM((HEADS_DEV, TOK, HEAD_DIM), bf),
            pltpu.VMEM((TOK, 3 * HEAD_DIM), f32),
            pltpu.VMEM((4, TOK, 2 * RANK), bf),
            pltpu.VMEM((3, TOK, 2 * RANK), bf),
            pltpu.VMEM((TOK, 2 * SLOTS * RANK), bf),
            pltpu.VMEM((TOK, 1), i32),
            pltpu.VMEM((TOK, 1), i32),
            dma((14, HEADS_DEV)),
            dma((14,)),
            dma((10,)),
            dma((10,)),
            dma((2,)),
            dma((2,)),
            dma((3,)),
            dma((3,)),
            dma,
            dma,
            dma((8,)),
            dma((3,)),
            dma((3,)),
        ],
        compiler_params=pltpu.CompilerParams(
            collective_id=0, has_side_effects=True, vmem_limit_bytes=67_043_328
        ),
    )(*operands)


def assemble(page_ref, k_ref, v_ref, out_ref):
    s = pl.program_id(0)
    offset, used = page_ref[s, 0], page_ref[s, 1]
    span = PAGE + 16
    first = jnp.minimum(offset // 16 * 16, KEEP - span)
    first = pl.multiple_of(first, 16)
    lines = jnp.concatenate([k_ref[pl.ds(first, span), :], v_ref[pl.ds(first, span), :]], axis=0)
    n = lax.broadcasted_iota(jnp.int32, (2 * PAGE, 2 * span), 0)
    m = lax.broadcasted_iota(jnp.int32, (2 * PAGE, 2 * span), 1)
    pick = (m == (n % 2) * span + n // 2 + (offset - first)) & (n // 2 < used)
    rows = jnp.dot(pick.astype(jnp.bfloat16), lines, preferred_element_type=jnp.float32)
    out_ref[0] = rows.astype(jnp.bfloat16).reshape(PAGE, 2, lines.shape[1])


def run_assemble(page, keys, values):
    wide = keys.shape[1]
    vmem = pl.BlockSpec(memory_space=pltpu.VMEM)
    return pl.pallas_call(
        assemble,
        grid=(SLOTS_DEV,),
        out_shape=jax.ShapeDtypeStruct((SLOTS_DEV, PAGE, 2, wide), keys.dtype),
        in_specs=[pl.BlockSpec(memory_space=pltpu.SMEM), vmem, vmem],
        out_specs=pl.BlockSpec((1, PAGE, 2, wide), lambda s: (s, 0, 0, 0)),
    )(page, keys, values)


def local(
    normed,
    projection_weight,
    adapter_down_weight,
    adapter_up_weight,
    packed_prompt_length,
    prompt_adapter_ids,
    slot_adapter_ids,
    prompt_page_slots,
):
    attended, keys, values, page = run_fused(
        normed.T,
        jnp.transpose(projection_weight, (1, 0, 2)),
        jnp.transpose(adapter_down_weight, (1, 2, 0))[0],
        adapter_up_weight,
        packed_prompt_length[None, :],
        prompt_adapter_ids[None, :],
        slot_adapter_ids[None, :],
        prompt_page_slots.T,
    )
    return attended, run_assemble(page, keys, values)


def solution(mesh):
    placed = (
        P(None, "col"),
        P("col", None, "row"),
        P(None, "col", None),
        P(None, None, None, "row"),
        P(),
        P(),
        P(),
        P(),
    )
    return jax.shard_map(
        local,
        mesh=mesh,
        in_specs=placed,
        out_specs=(P("col", "row"), P("col", None, None, "row")),
        check_vma=False,
    )
```

time: 312 us -> 217 us (0.70)
  the two profiles are of different devices: /device:TPU:3 before, /device:TPU:30 now
where the time goes in v2:
time: 217 us
  Pallas kernels  216 us (100%)
    pallas_call x1, Pallas kernels, run_fused(): pl.pallas_call(fused, out_shape=(jax.ShapeDtypeStruct((TOK, wide), bf), j...  207 us
    pallas_call x1, Pallas kernels, run_assemble(): pl.pallas_call(assemble, grid=(SLOTS_DEV,), out_shape=jax.ShapeDtypeStruc...  8.39 us

profile of v2, /device:TPU:30, one launch (start us, length us, event | category | flops | bytes accessed | tf_op | source)
XLA Modules:
  0.0 217.1 jit_solution(6380940144017070456)
XLA Ops:
  0.6 207.1 %shard_map.95 = (bf16[512,896]{1,0:T(8,128)(2,1)}, bf16[640,896]{1,0:T(8,128)(2,1)}, bf16[640,896]{1,0:T(8,128)(2,1)}, s32[16,128]{1,0:T(8,128)}) custom-call(bf16[448,8192]{1,0:T(8,128)(2,1)} %bitcast.9, bf16[3,448,896]{2,1,0:T(8,128)(2,1)} %bitcast.10, bf16[32,7168]{1,0:T(8,128)(2,1)} %bitcast.11, bf16[16,2,16,896]{3,2,1,0:T(8,128)(2,1)} %up_ref.1, ...), custom_call_target="tpu_custom_call" | custom-call | tf_op jit(solution)/shard_map/pallas_call | solution.py:546
  207.8 0.0 copy-start
  207.8 8.4 %shard_map.96 = bf16[10,128,2,896]{3,2,1,0:T(2,128)(2,1)} custom-call(s32[16,128]{1,0:T(8,128)} %get-tuple-element.7.page_ref, bf16[640,896]{1,0:T(8,128)(2,1)} %get-tuple-element.8.k_ref, bf16[640,896]{1,0:T(8,128)(2,1)} %get-tuple-element.9.v_ref), custom_call_target="tpu_custom_call" | custom-call | tf_op jit(solution)/shard_map/pallas_call | solution.py:609
  216.2 0.0 copy-done
  216.2 0.9 copy.11
Async XLA Ops:
  207.8 8.4 %copy-start = (bf16[512,896]{1,0:T(8,128)(2,1)S(1)}, bf16[512,896]{1,0:T(8,128)(2,1)}, u32[]{:S(2)}) copy-start(bf16[512,896]{1,0:T(8,128)(2,1)} %get-tuple-element.12) | copy-start | bytes 2752516

commit v3 on v2

--- a/solution.py
+++ b/solution.py
@@ -8,7 +8,9 @@
 HEAD_DIM = 128
 PAGE = 128
 SLOTS_DEV = 10
+PER_STEP = 2
 HEADS_DEV = 7
+KV_BLOCKS = 14
 SLOTS = 16
 RANK = 16
 TOK = 512
@@ -17,8 +19,8 @@
 BAND = 640
 PROMPTS = 64
 QUARTER = 128
-FAR = 128
-VIA = 400
+FAR = 224
+VIA = 432
 
 adapter_scale = 2.0
 masked_score = -1e30
@@ -143,7 +145,11 @@
 
     def w_own(h):
         for j in range(3):
-            src = w_ref.at[j, :, pl.ds(pl.multiple_of(h * HEAD_DIM, HEAD_DIM), HEAD_DIM)]
+            g = 3 * h + j
+            late = g // KV_BLOCKS
+            kind = (1 + g % 2) * (1 - late)
+            head = late * (g - KV_BLOCKS) + (1 - late) * (g // 2)
+            src = w_ref.at[kind, :, pl.ds(pl.multiple_of(head * HEAD_DIM, HEAD_DIM), HEAD_DIM)]
             lanes = pl.ds(j * HEAD_DIM, HEAD_DIM)
 
             @pl.when(lane0)
@@ -166,12 +172,14 @@
         yt = y + (n % 2) * (mate - y)
         tt = xt * 4 + yt + d * (3 - 2 * yt)
         first = pl.multiple_of(tt * TOK + z * QUARTER, QUARTER)
-        return xt, yt, pltpu.make_async_copy(
-            nt_ref.at[:, pl.ds(first, QUARTER)], raw.at[n], raws.at[n]
-        )
+        return xt, yt, first
+
+    def loading(n):
+        columns = pl.ds(block_of(n)[2], QUARTER)
+        return pltpu.make_async_copy(nt_ref.at[:, columns], raw.at[n], raws.at[n])
 
     def load(n, c):
-        block_of(n)[2].start()
+        loading(n).start()
         return c
 
     lax.fori_loop(0, 8, load, 0)
@@ -182,8 +190,8 @@
     ranks = pl.ds(pl.multiple_of(z * 8, 8), 8)
 
     def scatter(n, c):
-        xt, yt, copy = block_of(n)
-        copy.wait()
+        xt, yt, _ = block_of(n)
+        loading(n).wait()
         stage[n] = raw[n].T
         itself = (xt == x) & (n % 2 == 0)
 
@@ -195,6 +203,22 @@
         def _():
             rc(stage.at[n], nbuf.at[b_src, x, mine], nss.at[0], ns.at[0], dev(xt, yt, z, k)).start()
 
+        return c
+
+    @pl.when(lane0)
+    def _():
+        w_first(0)
+
+    lax.fori_loop(0, 8, scatter, 0)
+
+    @pl.when(lane1)
+    def _():
+        w_first(0)
+
+    def maps(n, c):
+        xt, yt, _ = block_of(n)
+        itself = (xt == x) & (n % 2 == 0)
+
         @pl.when((b_src == k) & itself)
         def _():
             pltpu.make_async_copy(at_ref.at[ranks], abuf.at[b_src, x], as_.at[0]).start()
@@ -205,15 +229,7 @@
 
         return c
 
-    @pl.when(lane0)
-    def _():
-        w_first(0)
-
-    lax.fori_loop(0, 8, scatter, 0)
-
-    @pl.when(lane1)
-    def _():
-        w_first(0)
+    lax.fori_loop(0, 8, maps, 0)
 
     @pl.when(lane0)
     def _():
@@ -274,6 +290,8 @@
         z1 = z + 1 - 2 * (z % 2)
         for s, to in enumerate((d_cross, dev(x, y, z1, k), dev(x, y, 3 - z, k))):
             rc(dpart.at[s], drecv.at[s], dss.at[s], ds_.at[s], to).start()
+            if s < 2:
+                mm(0, s)
             got(drecv.at[s], ds_.at[s])
             dpart[s + 1] = dpart[s] + drecv[s]
         rows = lax.broadcasted_iota(jnp.int32, (2 * RANK, 2 * SLOTS * RANK), 0)
@@ -283,6 +301,7 @@
         slot_at = (lax.broadcasted_iota(jnp.int32, (TOK, 2 * SLOTS * RANK), 1) // RANK) % SLOTS
         spread[...] = jnp.where(slot_at == tslot[...], wide, 0.0).astype(jnp.bfloat16)
         got(ubuf, us)
+        finish(0)
 
     def head_lanes(h):
         return pl.ds(pl.multiple_of(h * HEAD_DIM, HEAD_DIM), HEAD_DIM)
@@ -298,7 +317,7 @@
             def _():
                 rc(src, dst, oss.at[n], os_.at[n], d_swap).start()
 
-    def qkv(h, n):
+    def mm(h, n):
         def part(q):
             s = jnp.dot(nbuf[q, 0], wbuf[h, q, 0], preferred_element_type=f32)
             for xx in range(1, 4):
@@ -316,55 +335,60 @@
         got(wbuf.at[h, theirs(1 - n)], rs.at[8 + n, h])
         part(theirs(1 - n))
 
+    def qkv(h, n):
+        mm(h, n)
+
         @pl.when(n == 1)
         def _():
             finish(h)
 
-    def finish(h):
-        lanes = pl.ds(pl.multiple_of(h * HEAD_DIM, HEAD_DIM), HEAD_DIM)
+    def finish(r):
         half = SLOTS * RANK
-        up_q = ubuf[:, 0, :, lanes].reshape(half, HEAD_DIM)
-        up_v = ubuf[:, 1, :, lanes].reshape(half, HEAD_DIM)
-        dq = jnp.dot(spread[:, :half], up_q, preferred_element_type=f32)
-        dv = jnp.dot(spread[:, half:], up_v, preferred_element_type=f32)
-        qbuf[h] = (acc[:, :HEAD_DIM] + adapter_scale * dq).astype(jnp.bfloat16)
-        kvwin[h, TOK:, :HEAD_DIM] = acc[:, HEAD_DIM : 2 * HEAD_DIM].astype(jnp.bfloat16)
-        kvwin[h, TOK:, HEAD_DIM:] = (acc[:, 2 * HEAD_DIM :] + adapter_scale * dv).astype(jnp.bfloat16)
-
-        @pl.when(tok < 15)
-        def _():
-            rc(
-                kvwin.at[h, TOK:], kvwin.at[h, 0:TOK], ss.at[11], rs.at[11, h], holder(tok + 1, z, p)
-            ).start()
-
-        deliver(
-            (
-                (kvwin.at[h, TOK:, 0:HEAD_DIM], out_k.at[KEEP - TOK :, head_lanes(h)], 1),
-                (kvwin.at[h, TOK:, HEAD_DIM:], out_v.at[KEEP - TOK :, head_lanes(h)], 2),
-            )
-        )
+
+        def one(j, carry):
+            g = 3 * r + j
+            block = acc.at[:, head_lanes(j)]
+
+            @pl.when((g < KV_BLOCKS) & (g % 2 == 0))
+            def _():
+                kvwin[g // 2, TOK:, :HEAD_DIM] = block[...].astype(jnp.bfloat16)
+
+            @pl.when((g < KV_BLOCKS) & (g % 2 == 1))
+            def _():
+                h = g // 2
+                up_v = ubuf[:, 1, :, head_lanes(h)].reshape(half, HEAD_DIM)
+                dv = jnp.dot(spread[:, half:], up_v, preferred_element_type=f32)
+                kvwin[h, TOK:, HEAD_DIM:] = (block[...] + adapter_scale * dv).astype(jnp.bfloat16)
+
+                @pl.when(tok < 15)
+                def _():
+                    mine_ = kvwin.at[h, TOK:]
+                    theirs_ = kvwin.at[h, 0:TOK]
+                    rc(mine_, theirs_, ss.at[11], rs.at[11, h], holder(tok + 1, z, p)).start()
+
+                deliver(
+                    (
+                        (kvwin.at[h, TOK:, 0:HEAD_DIM], out_k.at[KEEP - TOK :, head_lanes(h)], 1),
+                        (kvwin.at[h, TOK:, HEAD_DIM:], out_v.at[KEEP - TOK :, head_lanes(h)], 2),
+                    )
+                )
+
+            @pl.when(g >= KV_BLOCKS)
+            def _():
+                h = g - KV_BLOCKS
+                up_q = ubuf[:, 0, :, head_lanes(h)].reshape(half, HEAD_DIM)
+                dq = jnp.dot(spread[:, :half], up_q, preferred_element_type=f32)
+                qbuf[...] = (block[...] + adapter_scale * dq).astype(jnp.bfloat16)
+                attend(h)
+
+            return carry
+
+        lax.fori_loop(0, 3, one, 0)
 
     def attend(h):
         @pl.when(tok > 0)
         def _():
             got(kvwin.at[h, 0:TOK], rs.at[11, h])
-
-        def block(i, carry):
-            r0 = pl.multiple_of(i * 128, 128)
-            qi = qbuf[h, pl.ds(r0, 128), :]
-            ki = kvwin[h, pl.ds(r0, BAND), :HEAD_DIM]
-            vi = kvwin[h, pl.ds(r0, BAND), HEAD_DIM:]
-            s = lax.dot_general(qi, ki, (((1,), (1,)), ((), ())), preferred_element_type=f32)
-            s = s * (HEAD_DIM**-0.5)
-            u = lax.broadcasted_iota(jnp.int32, (128, BAND), 1)
-            r = lax.broadcasted_iota(jnp.int32, (128, BAND), 0)
-            lo = low[pl.ds(r0, 128), :] - r0
-            s = jnp.where((u >= lo) & (u <= r + TOK), s, masked_score)
-            e = jnp.exp(s - jnp.max(s, axis=1, keepdims=True))
-            total = jnp.sum(e, axis=1, keepdims=True)
-            o = jnp.dot(e.astype(jnp.bfloat16), vi, preferred_element_type=f32)
-            att[h, pl.ds(r0, 128), :] = (o / total).astype(jnp.bfloat16)
-            return carry
 
         early = pl.ds(2 * TOK - KEEP, KEEP - TOK)
         deliver(
@@ -373,7 +397,22 @@
                 (kvwin.at[h, early, HEAD_DIM:], out_v.at[0 : KEEP - TOK, head_lanes(h)], 2),
             )
         )
-        lax.fori_loop(0, 4, block, 0)
+        for i in range(4):
+            r0 = i * 128
+            qi = qbuf[r0 : r0 + 128, :]
+            ki = kvwin[h, r0 : r0 + BAND, :HEAD_DIM]
+            vi = kvwin[h, r0 : r0 + BAND, HEAD_DIM:]
+            s = lax.dot_general(qi, ki, (((1,), (1,)), ((), ())), preferred_element_type=f32)
+            s = s * (HEAD_DIM**-0.5)
+            u = lax.broadcasted_iota(jnp.int32, (128, BAND), 1)
+            r = lax.broadcasted_iota(jnp.int32, (128, BAND), 0)
+            lo = low[r0 : r0 + 128, :] - r0
+            s = jnp.where((u >= lo) & (u <= r + TOK), s, masked_score)
+            e = jnp.exp(s - jnp.max(s, axis=1, keepdims=True))
+            total = jnp.sum(e, axis=1, keepdims=True)
+            o = jnp.dot(e.astype(jnp.bfloat16), vi, preferred_element_type=f32)
+            att[h, r0 : r0 + 128, :] = (o / total).astype(jnp.bfloat16)
+
         deliver(((att.at[h], out_att.at[:, head_lanes(h)], 0),))
 
     def tokens_of(zz):
@@ -423,12 +462,12 @@
             rc(u, nbuf.at[2:4, :, mine], nss.at[1], ns.at[1], d_cross).start()
             rc(u, u, nss.at[2], ns.at[2], d_zp).start()
             rc(u, u, nss.at[3], ns.at[3], d_zm).start()
+
+        @pl.when(i == 2)
+        def _():
+            u = nbuf.at[2:4, :, mine]
             got(abuf.at[k], as_.at[0])
             rc(abuf.at[k], abuf.at[k], ass.at[1], as_.at[1], d_core).start()
-
-        @pl.when(i == 2)
-        def _():
-            u = nbuf.at[2:4, :, mine]
             got(u, ns.at[1])
             rc(u, u, nss.at[4], ns.at[4], d_zp).start()
             rc(u, u, nss.at[5], ns.at[5], d_zm).start()
@@ -448,25 +487,17 @@
             u = nbuf.at[3, :, tokens_of(zp)]
             rc(u, u, nss.at[9], ns.at[9], d_zm).start()
 
-        @pl.when(i == 4)
+        @pl.when(i == 5)
         def _():
             for q in range(4):
                 got(nbuf.at[q, :, tokens_of(zf)], ns.at[6 + q])
             got(abuf.at[1 - k], as_.at[1])
             down()
 
-        @pl.when(i >= 5)
-        def _():
-            def one(h, c):
-                attend(h)
-                return c
-
-            lax.fori_loop(i - 4 - 6 // i, i - 3 - 6 // (i + 1), one, 0)
-
         def first_step(i):
-            return 2 * i - 5 - 6 // i - 2 * (5 // i)
-
-        @pl.when((i >= 4) & (i < HEADS_DEV + 3))
+            return 2 * i - 5 - 2 * (7 // i) - 2 * (6 // i) + (5 // i)
+
+        @pl.when((i >= 5) & (i < HEADS_DEV + 3))
         def _():
             def one(step, c):
                 @pl.when(step < 2 * HEADS_DEV)
@@ -490,7 +521,7 @@
 
         return carry
 
-    lax.fori_loop(0, HEADS_DEV + 4, round_, 0)
+    lax.fori_loop(0, HEADS_DEV + 3, round_, 0)
 
     for n in (0, 1, 2, 7):
         sent(wbuf.at[:, 0, 0], ss.at[n])
@@ -561,7 +592,7 @@
             pltpu.VMEM((8, WID, QUARTER), bf),
             pltpu.VMEM((8, QUARTER, WID), bf),
             pltpu.VMEM((HEADS_DEV, 2 * TOK, 2 * HEAD_DIM), bf),
-            pltpu.VMEM((HEADS_DEV, TOK, HEAD_DIM), bf),
+            pltpu.VMEM((TOK, HEAD_DIM), bf),
             pltpu.VMEM((HEADS_DEV, TOK, HEAD_DIM), bf),
             pltpu.VMEM((TOK, 3 * HEAD_DIM), f32),
             pltpu.VMEM((4, TOK, 2 * RANK), bf),
@@ -590,7 +621,11 @@
 
 
 def assemble(page_ref, k_ref, v_ref, out_ref):
-    s = pl.program_id(0)
+    for i in range(PER_STEP):
+        one_page(pl.program_id(0) * PER_STEP + i, i, page_ref, k_ref, v_ref, out_ref)
+
+
+def one_page(s, i, page_ref, k_ref, v_ref, out_ref):
     offset, used = page_ref[s, 0], page_ref[s, 1]
     span = PAGE + 16
     first = jnp.minimum(offset // 16 * 16, KEEP - span)
@@ -600,7 +635,7 @@
     m = lax.broadcasted_iota(jnp.int32, (2 * PAGE, 2 * span), 1)
     pick = (m == (n % 2) * span + n // 2 + (offset - first)) & (n // 2 < used)
     rows = jnp.dot(pick.astype(jnp.bfloat16), lines, preferred_element_type=jnp.float32)
-    out_ref[0] = rows.astype(jnp.bfloat16).reshape(PAGE, 2, lines.shape[1])
+    out_ref[i] = rows.astype(jnp.bfloat16).reshape(PAGE, 2, lines.shape[1])
 
 
 def run_assemble(page, keys, values):
@@ -608,10 +643,10 @@
     vmem = pl.BlockSpec(memory_space=pltpu.VMEM)
     return pl.pallas_call(
         assemble,
-        grid=(SLOTS_DEV,),
+        grid=(SLOTS_DEV // PER_STEP,),
         out_shape=jax.ShapeDtypeStruct((SLOTS_DEV, PAGE, 2, wide), keys.dtype),
         in_specs=[pl.BlockSpec(memory_space=pltpu.SMEM), vmem, vmem],
-        out_specs=pl.BlockSpec((1, PAGE, 2, wide), lambda s: (s, 0, 0, 0)),
+        out_specs=pl.BlockSpec((PER_STEP, PAGE, 2, wide), lambda s: (s, 0, 0, 0)),
     )(page, keys, values)
 
 

time: 217 us -> 206 us (0.949)
  the two profiles are of different devices: /device:TPU:30 before, /device:TPU:3 now
where the time goes in v3:
time: 206 us; the launch traced here: 205 us
  Pallas kernels  204 us (99%)
    pallas_call x1, Pallas kernels, run_fused(): pl.pallas_call(fused, out_shape=(jax.ShapeDtypeStruct((TOK, wide), bf), j...  197 us
    pallas_call x1, Pallas kernels, run_assemble(): pl.pallas_call(assemble, grid=(SLOTS_DEV // PER_STEP,), out_shape=jax.Sha...  6.83 us

profile of v3, /device:TPU:3, one launch (start us, length us, event | category | flops | bytes accessed | tf_op | source)
XLA Modules:
  0.0 205.1 jit_solution(12073803024236687670)
XLA Ops:
  0.6 196.7 %shard_map.95 = (bf16[512,896]{1,0:T(8,128)(2,1)}, bf16[640,896]{1,0:T(8,128)(2,1)}, bf16[640,896]{1,0:T(8,128)(2,1)}, s32[16,128]{1,0:T(8,128)}) custom-call(bf16[448,8192]{1,0:T(8,128)(2,1)} %bitcast.9, bf16[3,448,896]{2,1,0:T(8,128)(2,1)} %bitcast.10, bf16[32,7168]{1,0:T(8,128)(2,1)} %bitcast.11, bf16[16,2,16,896]{3,2,1,0:T(8,128)(2,1)} %up_ref.1, ...), custom_call_target="tpu_custom_call" | custom-call | tf_op jit(solution)/shard_map/pallas_call | solution.py:577
  197.3 0.0 copy-start
  197.3 6.8 %shard_map.96 = bf16[10,128,2,896]{3,2,1,0:T(2,128)(2,1)} custom-call(s32[16,128]{1,0:T(8,128)} %get-tuple-element.7.page_ref, bf16[640,896]{1,0:T(8,128)(2,1)} %get-tuple-element.8.k_ref, bf16[640,896]{1,0:T(8,128)(2,1)} %get-tuple-element.9.v_ref), custom_call_target="tpu_custom_call" | custom-call | tf_op jit(solution)/shard_map/pallas_call | solution.py:644
  204.2 0.0 copy-done
  204.2 0.9 copy.11
Async XLA Ops:
  197.3 6.8 %copy-start = (bf16[512,896]{1,0:T(8,128)(2,1)S(1)}, bf16[512,896]{1,0:T(8,128)(2,1)}, u32[]{:S(2)}) copy-start(bf16[512,896]{1,0:T(8,128)(2,1)} %get-tuple-element.12) | copy-start | bytes 2752516

commit v4 on v3

--- a/solution.py
+++ b/solution.py
@@ -141,9 +141,7 @@
 
     greet(holder((tok + 1) % 16, z, p))
     greet(holder((tok + 15) % 16, z, p))
-    pl.semaphore_wait(barrier, len(near) + 2)
-
-    def w_own(h):
+    def w_own(h, kind_of_lane=None):
         for j in range(3):
             g = 3 * h + j
             late = g // KV_BLOCKS
@@ -152,13 +150,17 @@
             src = w_ref.at[kind, :, pl.ds(pl.multiple_of(head * HEAD_DIM, HEAD_DIM), HEAD_DIM)]
             lanes = pl.ds(j * HEAD_DIM, HEAD_DIM)
 
-            @pl.when(lane0)
-            def _():
-                pltpu.make_async_copy(src, wbuf.at[h, q_own, x, :, lanes], rs.at[10, h]).start()
-
-            @pl.when(lane1)
-            def _():
-                rc(src, wbuf.at[h, 2 + b_src, x, :, lanes], ss.at[10], rs.at[10, h], d_swap).start()
+            if kind_of_lane in (None, 0):
+
+                @pl.when(lane0)
+                def _():
+                    pltpu.make_async_copy(src, wbuf.at[h, q_own, x, :, lanes], rs.at[10, h]).start()
+
+            if kind_of_lane in (None, 1):
+
+                @pl.when(lane1)
+                def _():
+                    rc(src, wbuf.at[h, 2 + b_src, x, :, lanes], ss.at[10], rs.at[10, h], d_swap).start()
 
     def w_first(h):
         own = wbuf.at[h, q_own, x]
@@ -183,58 +185,17 @@
         return c
 
     lax.fori_loop(0, 8, load, 0)
-    w_own(0)
-    w_own(1)
-    w_own(2)
+    for h in range(3):
+        w_own(h, 0)
     mine = pl.ds(pl.multiple_of(z * QUARTER, QUARTER), QUARTER)
     ranks = pl.ds(pl.multiple_of(z * 8, 8), 8)
 
-    def scatter(n, c):
-        xt, yt, _ = block_of(n)
+    def turn(n, c):
         loading(n).wait()
         stage[n] = raw[n].T
-        itself = (xt == x) & (n % 2 == 0)
-
-        @pl.when(itself)
-        def _():
-            pltpu.make_async_copy(stage.at[n], nbuf.at[b_src, x, mine], ns.at[0]).start()
-
-        @pl.when(jnp.logical_not(itself))
-        def _():
-            rc(stage.at[n], nbuf.at[b_src, x, mine], nss.at[0], ns.at[0], dev(xt, yt, z, k)).start()
-
         return c
 
-    @pl.when(lane0)
-    def _():
-        w_first(0)
-
-    lax.fori_loop(0, 8, scatter, 0)
-
-    @pl.when(lane1)
-    def _():
-        w_first(0)
-
-    def maps(n, c):
-        xt, yt, _ = block_of(n)
-        itself = (xt == x) & (n % 2 == 0)
-
-        @pl.when((b_src == k) & itself)
-        def _():
-            pltpu.make_async_copy(at_ref.at[ranks], abuf.at[b_src, x], as_.at[0]).start()
-
-        @pl.when((b_src == k) & jnp.logical_not(itself))
-        def _():
-            rc(at_ref.at[ranks], abuf.at[b_src, x], ass.at[0], as_.at[0], dev(xt, yt, z, k)).start()
-
-        return c
-
-    lax.fori_loop(0, 8, maps, 0)
-
-    @pl.when(lane0)
-    def _():
-        pltpu.make_async_copy(up_ref, ubuf, us).start()
-        rc(up_ref, ubuf, uss, us, d_core).start()
+    lax.fori_loop(0, 8, turn, 0)
 
     @pl.when(tok == 0)
     def _():
@@ -269,6 +230,55 @@
     offset = jnp.clip(offset.astype(jnp.int32) - base, 0, KEEP - 1)
     lane = lax.broadcasted_iota(jnp.int32, (SLOTS, 128), 1)
     out_page[...] = jnp.where(lane == 0, offset, used.astype(jnp.int32))
+
+    pl.semaphore_wait(barrier, len(near) + 2)
+    for h in range(3):
+        w_own(h, 1)
+
+    def scatter(n, c):
+        xt, yt, _ = block_of(n)
+        itself = (xt == x) & (n % 2 == 0)
+
+        @pl.when(itself)
+        def _():
+            pltpu.make_async_copy(stage.at[n], nbuf.at[b_src, x, mine], ns.at[0]).start()
+
+        @pl.when(jnp.logical_not(itself))
+        def _():
+            rc(stage.at[n], nbuf.at[b_src, x, mine], nss.at[0], ns.at[0], dev(xt, yt, z, k)).start()
+
+        return c
+
+    @pl.when(lane0)
+    def _():
+        w_first(0)
+
+    lax.fori_loop(0, 8, scatter, 0)
+
+    @pl.when(lane1)
+    def _():
+        w_first(0)
+
+    def maps(n, c):
+        xt, yt, _ = block_of(n)
+        itself = (xt == x) & (n % 2 == 0)
+
+        @pl.when((b_src == k) & itself)
+        def _():
+            pltpu.make_async_copy(at_ref.at[ranks], abuf.at[b_src, x], as_.at[0]).start()
+
+        @pl.when((b_src == k) & jnp.logical_not(itself))
+        def _():
+            rc(at_ref.at[ranks], abuf.at[b_src, x], ass.at[0], as_.at[0], dev(xt, yt, z, k)).start()
+
+        return c
+
+    lax.fori_loop(0, 8, maps, 0)
+
+    @pl.when(lane0)
+    def _():
+        pltpu.make_async_copy(up_ref, ubuf, us).start()
+        rc(up_ref, ubuf, uss, us, d_core).start()
 
     def down():
         total = jnp.zeros((TOK, 64), f32)
@@ -463,7 +473,7 @@
             rc(u, u, nss.at[2], ns.at[2], d_zp).start()
             rc(u, u, nss.at[3], ns.at[3], d_zm).start()
 
-        @pl.when(i == 2)
+        @pl.when(i == 1)
         def _():
             u = nbuf.at[2:4, :, mine]
             got(abuf.at[k], as_.at[0])
@@ -478,7 +488,7 @@
             u = nbuf.at[1, :, tokens_of(zp)]
             rc(u, u, nss.at[7], ns.at[7], d_zm).start()
 
-        @pl.when(i == 3)
+        @pl.when(i == 2)
         def _():
             got(nbuf.at[2:4, :, tokens_of(zm)], ns.at[4])
             u = nbuf.at[2, :, tokens_of(zm)]
@@ -487,7 +497,7 @@
             u = nbuf.at[3, :, tokens_of(zp)]
             rc(u, u, nss.at[9], ns.at[9], d_zm).start()
 
-        @pl.when(i == 5)
+        @pl.when(i == 4)
         def _():
             for q in range(4):
                 got(nbuf.at[q, :, tokens_of(zf)], ns.at[6 + q])
@@ -495,9 +505,9 @@
             down()
 
         def first_step(i):
-            return 2 * i - 5 - 2 * (7 // i) - 2 * (6 // i) + (5 // i)
-
-        @pl.when((i >= 5) & (i < HEADS_DEV + 3))
+            return 2 * i - 5 - 4 // i
+
+        @pl.when((i >= 4) & (i < HEADS_DEV + 3))
         def _():
             def one(step, c):
                 @pl.when(step < 2 * HEADS_DEV)

time: 206 us -> 202 us (0.981)
  Pallas kernels: 204 us -> 200 us
    pallas_call x1, Pallas kernels: 197 us -> 193 us  [run_fused(): pl.pallas_call(fused, out_shape=(jax.ShapeDtypeStruct((TOK, wide), bf), j...]
where the time goes in v4:
time: 202 us
  Pallas kernels  200 us (99%)
    pallas_call x1, Pallas kernels, run_fused(): pl.pallas_call(fused, out_shape=(jax.ShapeDtypeStruct((TOK, wide), bf), j...  193 us
    pallas_call x1, Pallas kernels, run_assemble(): pl.pallas_call(assemble, grid=(SLOTS_DEV // PER_STEP,), out_shape=jax.Sha...  6.82 us

profile of v4, /device:TPU:3, one launch (start us, length us, event | category | flops | bytes accessed | tf_op | source)
XLA Modules:
  0.0 201.7 jit_solution(3305354181007626290)
XLA Ops:
  0.6 193.3 %shard_map.95 = (bf16[512,896]{1,0:T(8,128)(2,1)}, bf16[640,896]{1,0:T(8,128)(2,1)}, bf16[640,896]{1,0:T(8,128)(2,1)}, s32[16,128]{1,0:T(8,128)}) custom-call(bf16[448,8192]{1,0:T(8,128)(2,1)} %bitcast.9, bf16[3,448,896]{2,1,0:T(8,128)(2,1)} %bitcast.10, bf16[32,7168]{1,0:T(8,128)(2,1)} %bitcast.11, bf16[16,2,16,896]{3,2,1,0:T(8,128)(2,1)} %up_ref.1, ...), custom_call_target="tpu_custom_call" | custom-call | tf_op jit(solution)/shard_map/pallas_call | solution.py:587
  194.0 0.0 copy-start
  194.0 6.8 %shard_map.96 = bf16[10,128,2,896]{3,2,1,0:T(2,128)(2,1)} custom-call(s32[16,128]{1,0:T(8,128)} %get-tuple-element.7.page_ref, bf16[640,896]{1,0:T(8,128)(2,1)} %get-tuple-element.8.k_ref, bf16[640,896]{1,0:T(8,128)(2,1)} %get-tuple-element.9.v_ref), custom_call_target="tpu_custom_call" | custom-call | tf_op jit(solution)/shard_map/pallas_call | solution.py:654
  200.8 0.0 copy-done
  200.8 0.9 copy.11
Async XLA Ops:
  194.0 6.8 %copy-start = (bf16[512,896]{1,0:T(8,128)(2,1)S(1)}, bf16[512,896]{1,0:T(8,128)(2,1)}, u32[]{:S(2)}) copy-start(bf16[512,896]{1,0:T(8,128)(2,1)} %get-tuple-element.12) | copy-start | bytes 2752516
